TPU v7x, 512 devices: a whole 4x8x8 slice. The times are simulated.
512 devices in a mesh: gx: 32 (over x, z), gy: 4 (over y_lo), chaos: 4 (over y_hi, core).
Axes of the slice: x: 4, y: 8 (y_hi: 2, y_lo: 4; y = y_hi * 4 + y_lo), z: 8, core: 2. Of those that a mesh axis runs over, the one named last changes fastest.
Arguments:
- field: float32 [68, 128, 32, 128], P('chaos', 'gx', 'gy'), may hold values from -6 to 6
- source: float32 [68, 128, 32, 128], P('chaos', 'gx', 'gy'), may hold values from -6 to 6
- mean_coef: float32 [128, 32, 128], P('gx', 'gy'), may hold values from 1 to 3
- var_coefs: float32 [10, 128, 32, 128], P(None, 'gx', 'gy'), may hold values from -0.6 to 0.6
- galerkin_cols: int32 [10, 68, 3], replicated, may hold values from 0 to 65
- galerkin_vals: float32 [10, 68, 3], replicated, may hold values from -3 to 3
Outputs:
- smoothed: float32 [68, 128, 32, 128], P('chaos', 'gx', 'gy')
- coarse_residual: float32 [68, 64, 16, 64], P('chaos', 'gx', 'gy')
All inputs are finite; a program needn't handle non-finite values.
Results may differ from a plain program's by a relative error of at most 0.0001.
Values sent between devices are 32-bit elements; how exact they have to be, the bound alone decides.
A program may use at most 128 MiB of HBM per device.

v0:
```python
import jax
import jax.numpy as jnp
from jax import lax
from jax.sharding import PartitionSpec as P

P_SIZE = 66


def padded_2(array, sides, width):
    edges = {}
    for axis, dim in sides:
        size, length = (lax.axis_size(axis), array.shape[dim])
        up = [(i, (i + 1) % size) for i in range(size - 1)]
        last = lax.slice_in_dim(array, length - width, length, axis=dim)
        initial = lax.slice_in_dim(array, 0, width, axis=dim)
        edges[dim] = (
            lax.ppermute(last, axis, up),
            lax.ppermute(initial, axis, [(b, a) for a, b in up]),
        )
    done = []
    for _, dim in sides:
        low, high = edges[dim]
        around = [(width, width) if d in done else (0, 0) for d in range(array.ndim)]
        array = jnp.concatenate([jnp.pad(low, around), array, jnp.pad(high, around)], axis=dim)
        done.append(dim)
    return array


def cut_along(array, dim, length):
    shape = array.shape
    pieces = array.reshape(*shape[:dim], length, shape[dim] // length, *shape[dim + 1 :])
    return jnp.moveaxis(pieces, dim, 0)


def sum_at_owner(array, axis, dim):
    pieces = cut_along(array, dim, lax.axis_size(axis))
    arrived = lax.all_to_all(pieces, axis, split_axis=0, concat_axis=0, tiled=True)
    return arrived.sum(axis=0)


def shifted(array, axis, by):
    length = lax.axis_size(axis)
    pairs = [(i, i + by) for i in range(length) if 0 <= i + by < length]
    return lax.ppermute(array, axis, pairs)


def build_mixing(galerkin_cols, galerkin_vals):
    slots = galerkin_cols.shape[1]
    match = (galerkin_cols[..., None] == jnp.arange(slots, dtype=jnp.int32)).astype(jnp.float32)
    return jnp.sum(match * galerkin_vals[..., None], axis=2)


def halve_local(values, axis, below):
    even = lax.slice_in_dim(values, 0, values.shape[axis], 2, axis)
    odd = lax.slice_in_dim(values, 1, values.shape[axis], 2, axis)
    lower = lax.slice_in_dim(odd, 0, odd.shape[axis] - 1, 1, axis)
    prev = jnp.concatenate([below, lower], axis)
    return 0.5 * even + 0.25 * (odd + prev)


def body(field, source, mean_coef, var_coefs, galerkin_cols, galerkin_vals):
    slots = field.shape[0]
    total = galerkin_cols.shape[1]
    first_row = lax.axis_index("chaos") * slots
    rows_global = first_row + jnp.arange(slots, dtype=jnp.int32)
    mask = (rows_global < P_SIZE).astype(jnp.float32)[:, None, None, None]
    mixing = build_mixing(galerkin_cols, galerkin_vals)
    terms = mixing.shape[0]
    cells = field.shape[1] * field.shape[2] * field.shape[3]
    own_cols = lax.dynamic_slice_in_dim(mixing, first_row, slots, 2)
    col_table = jnp.transpose(own_cols, (1, 0, 2)).reshape(total, terms * slots)

    def operate(values):
        padded = padded_2(values, (("gx", 1), ("gy", 2)), 1)
        zeros_plane = jnp.zeros_like(values[:, :, :, :1])
        beside = padded[:, 2:, 1:-1, :] + padded[:, :-2, 1:-1, :]
        beside = beside + padded[:, 1:-1, 2:, :] + padded[:, 1:-1, :-2, :]
        beside = beside + jnp.concatenate([values[:, :, :, 1:], zeros_plane], 3)
        beside = beside + jnp.concatenate([zeros_plane, values[:, :, :, :-1]], 3)
        lap = 6.0 * values - beside
        scaled = (var_coefs[:, None] * lap[None]).reshape(terms * slots, cells)
        coupled = sum_at_owner(
            jnp.dot(col_table, scaled, precision=lax.Precision.HIGHEST), "chaos", 0
        )
        return mean_coef[None] * lap + coupled.reshape(values.shape)

    start_field = mask * field
    first = source - operate(start_field)
    smoothed = mask * (start_field + 2.0 / 3.0 * first / (6.0 * mean_coef[None]))
    after = mask * (source - operate(smoothed))
    below_x = shifted(after[:, -1:], "gx", 1)
    coarse = halve_local(after, 1, below_x)
    below_y = shifted(coarse[:, :, -1:], "gy", 1)
    coarse = halve_local(coarse, 2, below_y)
    coarse = halve_local(coarse, 3, jnp.zeros_like(coarse[:, :, :, :1]))
    return (smoothed, coarse)


def solution(mesh):
    return jax.shard_map(
        body,
        mesh=mesh,
        in_specs=(
            P("chaos", "gx", "gy", None),
            P("chaos", "gx", "gy", None),
            P("gx", "gy", None),
            P(None, "gx", "gy", None),
            P(),
            P(),
        ),
        out_specs=(P("chaos", "gx", "gy", None), P("chaos", "gx", "gy", None)),
        check_vma=False,
    )
```

profile of v0, /device:TPU:22, one launch (start us, length us, event | category | flops | bytes accessed | tf_op | source)
XLA Modules:
  0.0 165.1 jit_solution(18192878544937780247)
XLA Ops:
  0.7 1.0 broadcast_multiply_fusion.2
  1.8 2.5 %collective-permute-start.2 = (f32[17,4,1,128]{3,2,1,0:T(1,128)S(1)}, f32[17,4,1,128]{3,2,1,0:T(1,128)S(1)}, u32[]{:S(2)}, u32[]{:S(2)}) collective-permute-start(f32[17,4,1,128]{3,2,1,0:T(1,128)S(1)} %get-tuple-element.10), channel_id=1, source_target_pairs={{4,0},{8,4},{12,8},{5,1},{9,5},{13,9},{6,2},{10,6},{14,10},{7,3},{... | collective-permute-start | bytes 104456 | tf_op jit(solution)/shard_map/ppermute | solution.py:18
  4.3 3.5 %collective-permute-start.3 = (f32[17,4,1,128]{3,2,1,0:T(1,128)S(1)}, f32[17,4,1,128]{3,2,1,0:T(1,128)S(1)}, u32[]{:S(2)}, u32[]{:S(2)}) collective-permute-start(f32[17,4,1,128]{3,2,1,0:T(1,128)S(1)} %get-tuple-element.11), channel_id=1, source_target_pairs={{0,4},{4,8},{8,12},{1,5},{5,9},{9,13},{2,6},{6,10},{10,14},{3,7},{... | collective-permute-start | bytes 104456 | tf_op jit(solution)/shard_map/ppermute | solution.py:17
  7.8 4.3 %collective-permute-start.1 = (f32[17,1,8,128]{3,2,1,0:T(8,128)S(1)}, f32[17,1,8,128]{3,2,1,0:T(8,128)S(1)}, u32[]{:S(2)}, u32[]{:S(2)}) collective-permute-start(f32[17,1,8,128]{3,2,1,0:T(8,128)S(1)} %get-tuple-element.12), channel_id=1, source_target_pairs={{0,16},{16,32},{32,48},{48,64},{64,80},{80,96},{96,112},{112,128},... | collective-permute-start | bytes 208904 | tf_op jit(solution)/shard_map/ppermute | solution.py:17
  12.1 8.9 %collective-permute-start = (f32[17,1,8,128]{3,2,1,0:T(8,128)S(1)}, f32[17,1,8,128]{3,2,1,0:T(8,128)S(1)}, u32[]{:S(2)}, u32[]{:S(2)}) collective-permute-start(f32[17,1,8,128]{3,2,1,0:T(8,128)S(1)} %get-tuple-element.13), channel_id=1, source_target_pairs={{16,0},{32,16},{48,32},{64,48},{80,64},{96,80},{112,96},{128,112},... | collective-permute-start | bytes 208904 | tf_op jit(solution)/shard_map/ppermute | solution.py:18
  21.1 1.5 select_reduce_fusion
  23.4 0.2 fusion.19
  23.6 1.9 %broadcast_multiply_fusion.1 = f32[10,17,4,8,128]{4,3,2,1,0:T(8,128)} fusion(f32[17,4,8,128]{3,2,1,0:T(8,128)S(1)} %fusion.19, f32[10,4,8,128]{3,2,1,0:T(8,128)S(1)} %copy-done.3), kind=kLoop, calls=%fused_computation.1 | loop fusion | flops 696320 | bytes 3227648 | tf_op jit(solution)/shard_map/mul | solution.py:81
  25.5 2.7 %reshape.59 = f32[170,4096,1]{1,0,2:T(8,128)S(1)} reshape(f32[10,17,4,8,128]{4,3,2,1,0:T(8,128)} %broadcast_multiply_fusion.1) | data formatting | bytes 5570560 | tf_op jit(solution)/shard_map/mul | solution.py:81
  28.2 2.8 %fusion.33 = f32[4,17,4096]{2,1,0:T(8,128)} fusion(f32[4,17,170]{2,1,0:T(8,128)S(1)} %copy.15, f32[170,4096,1]{1,0,2:T(8,128)S(1)} %reshape.59), kind=kOutput, calls=%fused_computation.64 | convolution fusion | flops 568197120 | bytes 3945632 | tf_op jit(solution)/shard_map/dot_general | solution.py:83
  31.1 5.4 %all-to-all-start = ((f32[4,17,4096]{2,1,0:T(8,128)}), f32[4,17,4096]{2,1,0:T(8,128)S(1)}, u32[]{:S(2)}, u32[]{:S(2)}) async-start(f32[4,17,4096]{2,1,0:T(8,128)} %fusion.33), calls=%async_computation | async-start | bytes 3145728 | tf_op jit(solution)/shard_map/all_to_all | solution.py:37
  36.5 40.7 %all-to-all-done = f32[4,17,4096]{2,1,0:T(8,128)S(1)} async-done(((f32[4,17,4096]{2,1,0:T(8,128)}), f32[4,17,4096]{2,1,0:T(8,128)S(1)}, u32[]{:S(2)}, u32[]{:S(2)}) %all-to-all-start) | async-done | bytes 1114144 | tf_op jit(solution)/shard_map/all_to_all | solution.py:37
  77.4 1.1 fusion.6
  78.6 2.3 %collective-permute-start.6 = (f32[17,4,1,128]{3,2,1,0:T(1,128)S(1)}, f32[17,4,1,128]{3,2,1,0:T(1,128)S(1)}, u32[]{:S(2)}, u32[]{:S(2)}) collective-permute-start(f32[17,4,1,128]{3,2,1,0:T(1,128)S(1)} %get-tuple-element.4), channel_id=1, source_target_pairs={{4,0},{8,4},{12,8},{5,1},{9,5},{13,9},{6,2},{10,6},{14,10},{7,3},{... | collective-permute-start | bytes 104456 | tf_op jit(solution)/shard_map/ppermute | solution.py:18
  80.9 3.6 %collective-permute-start.7 = (f32[17,4,1,128]{3,2,1,0:T(1,128)S(1)}, f32[17,4,1,128]{3,2,1,0:T(1,128)S(1)}, u32[]{:S(2)}, u32[]{:S(2)}) collective-permute-start(f32[17,4,1,128]{3,2,1,0:T(1,128)S(1)} %get-tuple-element.5), channel_id=1, source_target_pairs={{0,4},{4,8},{8,12},{1,5},{5,9},{9,13},{2,6},{6,10},{10,14},{3,7},{... | collective-permute-start | bytes 104456 | tf_op jit(solution)/shard_map/ppermute | solution.py:17
  84.4 1.9 %collective-permute-start.5 = (f32[17,1,8,128]{3,2,1,0:T(8,128)S(1)}, f32[17,1,8,128]{3,2,1,0:T(8,128)S(1)}, u32[]{:S(2)}, u32[]{:S(2)}) collective-permute-start(f32[17,1,8,128]{3,2,1,0:T(8,128)S(1)} %get-tuple-element.6), channel_id=1, source_target_pairs={{0,16},{16,32},{32,48},{48,64},{64,80},{80,96},{96,112},{112,128},... | collective-permute-start | bytes 208904 | tf_op jit(solution)/shard_map/ppermute | solution.py:17
  86.3 6.0 %collective-permute-start.4 = (f32[17,1,8,128]{3,2,1,0:T(8,128)S(1)}, f32[17,1,8,128]{3,2,1,0:T(8,128)S(1)}, u32[]{:S(2)}, u32[]{:S(2)}) collective-permute-start(f32[17,1,8,128]{3,2,1,0:T(8,128)S(1)} %get-tuple-element.7), channel_id=1, source_target_pairs={{16,0},{32,16},{48,32},{64,48},{80,64},{96,80},{112,96},{128,112},... | collective-permute-start | bytes 208904 | tf_op jit(solution)/shard_map/ppermute | solution.py:18
  92.7 1.6 collective-permute-done.4
  94.3 0.2 fusion.11
  94.5 1.9 %broadcast_multiply_fusion = f32[10,17,4,8,128]{4,3,2,1,0:T(8,128)} fusion(f32[17,4,8,128]{3,2,1,0:T(8,128)S(1)} %fusion.11, f32[10,4,8,128]{3,2,1,0:T(8,128)S(1)} %copy-done.4), kind=kLoop, calls=%fused_computation | loop fusion | flops 696320 | bytes 3227648 | tf_op jit(solution)/shard_map/mul | solution.py:81
  96.4 2.7 %reshape.60 = f32[170,4096,1]{1,0,2:T(8,128)S(1)} reshape(f32[10,17,4,8,128]{4,3,2,1,0:T(8,128)} %broadcast_multiply_fusion) | data formatting | bytes 5570560 | tf_op jit(solution)/shard_map/mul | solution.py:81
  99.2 1.7 %fusion.34 = f32[4,17,4096]{2,1,0:T(8,128)S(1)} fusion(f32[4,17,170]{2,1,0:T(8,128)S(1)} %copy.15, f32[170,4096,1]{1,0,2:T(8,128)S(1)} %reshape.60), kind=kOutput, calls=%fused_computation.65 | convolution fusion | flops 568197120 | bytes 3945632 | tf_op jit(solution)/shard_map/dot_general | solution.py:83
  100.9 43.4 %all_to_all.10 = f32[4,17,4096]{2,1,0:T(8,128)S(1)} all-to-all(f32[4,17,4096]{2,1,0:T(8,128)S(1)} %fusion.34), channel_id=1, replica_groups=mesh['gx'=32,'gy'=4,'chaos'=4] {'chaos'}, dimensions={0} | all-to-all | bytes 2228224 | tf_op jit(solution)/shard_map/all_to_all | solution.py:37
  144.6 2.6 %collective-permute-start.8 = (f32[17,1,8,128]{3,2,1,0:T(8,128)S(1)}, f32[17,1,8,128]{3,2,1,0:T(8,128)S(1)}, u32[]{:S(2)}, u32[]{:S(2)}) collective-permute-start(f32[17,1,8,128]{3,2,1,0:T(8,128)S(1)} %slice.144), channel_id=1, source_target_pairs={{0,16},{16,32},{32,48},{48,64},{64,80},{80,96},{96,112},{112,128},... | collective-permute-start | bytes 208904 | tf_op jit(solution)/shard_map/ppermute | solution.py:44
  147.2 6.1 %collective-permute-done.8 = f32[17,1,8,128]{3,2,1,0:T(8,128)S(1)} collective-permute-done((f32[17,1,8,128]{3,2,1,0:T(8,128)S(1)}, f32[17,1,8,128]{3,2,1,0:T(8,128)S(1)}, u32[]{:S(2)}, u32[]{:S(2)}) %collective-permute-start.8) | collective-permute-done | bytes 69664 | tf_op jit(solution)/shard_map/ppermute | solution.py:44
  153.3 1.9 %collective-permute-start.9 = (f32[17,2,1,128]{3,2,1,0:T(1,128)S(1)}, f32[17,2,1,128]{3,2,1,0:T(1,128)S(1)}, u32[]{:S(2)}, u32[]{:S(2)}) collective-permute-start(f32[17,2,1,128]{3,2,1,0:T(1,128)S(1)} %slice.146), channel_id=1, source_target_pairs={{0,4},{4,8},{8,12},{1,5},{5,9},{9,13},{2,6},{6,10},{10,14},{3,7},{... | collective-permute-start | bytes 52232 | tf_op jit(solution)/shard_map/ppermute | solution.py:44
  155.2 0.4 slice.126
  155.6 0.4 slice.125
  156.0 2.9 %collective-permute-done.9 = f32[17,2,1,128]{3,2,1,0:T(1,128)S(1)} collective-permute-done((f32[17,2,1,128]{3,2,1,0:T(1,128)S(1)}, f32[17,2,1,128]{3,2,1,0:T(1,128)S(1)}, u32[]{:S(2)}, u32[]{:S(2)}) %collective-permute-start.9) | collective-permute-done | bytes 17440 | tf_op jit(solution)/shard_map/ppermute | solution.py:44
  159.0 2.7 %slice.130 = f32[17,2,4,64]{3,2,1,0:T(4,128)S(1)} slice(f32[17,2,4,128]{3,2,1,0:T(4,128)S(1)} %fusion.26), slice={[0:17:1], [0:2:1], [0:4:1], [1:128:2]} | slice | bytes 69632 | tf_op jit(solution)/shard_map/slice | solution.py:55
  161.7 2.6 %slice.129 = f32[17,2,4,64]{3,2,1,0:T(4,128)S(1)} slice(f32[17,2,4,128]{3,2,1,0:T(4,128)S(1)} %fusion.26), slice={[0:17:1], [0:2:1], [0:4:1], [0:128:2]} | slice | bytes 69632 | tf_op jit(solution)/shard_map/slice | solution.py:54
  164.3 0.7 multiply_add_fusion
  (48 shorter events, 2.0 us)
Async XLA Ops:
  0.6 11.4 %copy-start.6 = (f32[17]{0:T(128)}, f32[17]{0:T(128)S(1)}, u32[]{:S(2)}) copy-start(f32[17]{0:T(128)S(1)} %compare_convert_fusion) | copy-start | bytes 208
  1.7 21.9 %copy-start.3 = (f32[10,4,8,128]{3,2,1,0:T(8,128)S(1)}, f32[10,4,8,128]{3,2,1,0:T(8,128)}, u32[]{:S(2)}) copy-start(f32[10,4,8,128]{3,2,1,0:T(8,128)} %param.9) | copy-start | bytes 491524
  1.8 21.6 %collective-permute-start.2 = (f32[17,4,1,128]{3,2,1,0:T(1,128)S(1)}, f32[17,4,1,128]{3,2,1,0:T(1,128)S(1)}, u32[]{:S(2)}, u32[]{:S(2)}) collective-permute-start(f32[17,4,1,128]{3,2,1,0:T(1,128)S(1)} %get-tuple-element.10), channel_id=1, source_target_pairs={{4,0},{8,4},{12,8},{5,1},{9,5},{13,9},{6,2},{10,6},{14,10},{7,3},{... | collective-permute-start | bytes 104456 | tf_op jit(solution)/shard_map/ppermute | solution.py:18
  4.3 19.1 %collective-permute-start.3 = (f32[17,4,1,128]{3,2,1,0:T(1,128)S(1)}, f32[17,4,1,128]{3,2,1,0:T(1,128)S(1)}, u32[]{:S(2)}, u32[]{:S(2)}) collective-permute-start(f32[17,4,1,128]{3,2,1,0:T(1,128)S(1)} %get-tuple-element.11), channel_id=1, source_target_pairs={{0,4},{4,8},{8,12},{1,5},{5,9},{9,13},{2,6},{6,10},{10,14},{3,7},{... | collective-permute-start | bytes 104456 | tf_op jit(solution)/shard_map/ppermute | solution.py:17
  7.8 15.6 %collective-permute-start.1 = (f32[17,1,8,128]{3,2,1,0:T(8,128)S(1)}, f32[17,1,8,128]{3,2,1,0:T(8,128)S(1)}, u32[]{:S(2)}, u32[]{:S(2)}) collective-permute-start(f32[17,1,8,128]{3,2,1,0:T(8,128)S(1)} %get-tuple-element.12), channel_id=1, source_target_pairs={{0,16},{16,32},{32,48},{48,64},{64,80},{80,96},{96,112},{112,128},... | collective-permute-start | bytes 208904 | tf_op jit(solution)/shard_map/ppermute | solution.py:17
  12.1 11.3 %collective-permute-start = (f32[17,1,8,128]{3,2,1,0:T(8,128)S(1)}, f32[17,1,8,128]{3,2,1,0:T(8,128)S(1)}, u32[]{:S(2)}, u32[]{:S(2)}) collective-permute-start(f32[17,1,8,128]{3,2,1,0:T(8,128)S(1)} %get-tuple-element.13), channel_id=1, source_target_pairs={{16,0},{32,16},{48,32},{64,48},{80,64},{96,80},{112,96},{128,112},... | collective-permute-start | bytes 208904 | tf_op jit(solution)/shard_map/ppermute | solution.py:18
  28.2 8.3 %copy-start.5 = (f32[4,8,128]{2,1,0:T(8,128)S(1)}, f32[4,8,128]{2,1,0:T(8,128)}, u32[]{:S(2)}) copy-start(f32[4,8,128]{2,1,0:T(8,128)} %param.8) | copy-start | bytes 49156
  31.1 46.3 %copy-start.1 = (f32[17,4,8,128]{3,2,1,0:T(8,128)S(1)}, f32[17,4,8,128]{3,2,1,0:T(8,128)}, u32[]{:S(2)}) copy-start(f32[17,4,8,128]{3,2,1,0:T(8,128)} %param.6) | copy-start | bytes 835588
  31.1 46.3 %copy-start.7 = (f32[17]{0:T(128)S(1)}, f32[17]{0:T(128)}, u32[]{:S(2)}) copy-start(f32[17]{0:T(128)} %copy-done.6) | copy-start | bytes 208
  31.1 46.1 %all-to-all-start = ((f32[4,17,4096]{2,1,0:T(8,128)}), f32[4,17,4096]{2,1,0:T(8,128)S(1)}, u32[]{:S(2)}, u32[]{:S(2)}) async-start(f32[4,17,4096]{2,1,0:T(8,128)} %fusion.33), calls=%async_computation | async-start | bytes 3145728 | tf_op jit(solution)/shard_map/all_to_all | solution.py:37
  77.3 17.2 %copy-start.4 = (f32[10,4,8,128]{3,2,1,0:T(8,128)S(1)}, f32[10,4,8,128]{3,2,1,0:T(8,128)}, u32[]{:S(2)}) copy-start(f32[10,4,8,128]{3,2,1,0:T(8,128)} %param.9) | copy-start | bytes 491524
  78.5 18.0 %copy-start = (f32[17,4,8,128]{3,2,1,0:T(8,128)}, f32[17,4,8,128]{3,2,1,0:T(8,128)S(1)}, u32[]{:S(2)}) copy-start(f32[17,4,8,128]{3,2,1,0:T(8,128)S(1)} %fusion.6) | copy-start | bytes 835588
  78.6 14.0 %collective-permute-start.6 = (f32[17,4,1,128]{3,2,1,0:T(1,128)S(1)}, f32[17,4,1,128]{3,2,1,0:T(1,128)S(1)}, u32[]{:S(2)}, u32[]{:S(2)}) collective-permute-start(f32[17,4,1,128]{3,2,1,0:T(1,128)S(1)} %get-tuple-element.4), channel_id=1, source_target_pairs={{4,0},{8,4},{12,8},{5,1},{9,5},{13,9},{6,2},{10,6},{14,10},{7,3},{... | collective-permute-start | bytes 104456 | tf_op jit(solution)/shard_map/ppermute | solution.py:18
  80.9 11.7 %collective-permute-start.7 = (f32[17,4,1,128]{3,2,1,0:T(1,128)S(1)}, f32[17,4,1,128]{3,2,1,0:T(1,128)S(1)}, u32[]{:S(2)}, u32[]{:S(2)}) collective-permute-start(f32[17,4,1,128]{3,2,1,0:T(1,128)S(1)} %get-tuple-element.5), channel_id=1, source_target_pairs={{0,4},{4,8},{8,12},{1,5},{5,9},{9,13},{2,6},{6,10},{10,14},{3,7},{... | collective-permute-start | bytes 104456 | tf_op jit(solution)/shard_map/ppermute | solution.py:17
  84.4 8.3 %collective-permute-start.5 = (f32[17,1,8,128]{3,2,1,0:T(8,128)S(1)}, f32[17,1,8,128]{3,2,1,0:T(8,128)S(1)}, u32[]{:S(2)}, u32[]{:S(2)}) collective-permute-start(f32[17,1,8,128]{3,2,1,0:T(8,128)S(1)} %get-tuple-element.6), channel_id=1, source_target_pairs={{0,16},{16,32},{32,48},{48,64},{64,80},{80,96},{96,112},{112,128},... | collective-permute-start | bytes 208904 | tf_op jit(solution)/shard_map/ppermute | solution.py:17
  86.3 8.0 %collective-permute-start.4 = (f32[17,1,8,128]{3,2,1,0:T(8,128)S(1)}, f32[17,1,8,128]{3,2,1,0:T(8,128)S(1)}, u32[]{:S(2)}, u32[]{:S(2)}) collective-permute-start(f32[17,1,8,128]{3,2,1,0:T(8,128)S(1)} %get-tuple-element.7), channel_id=1, source_target_pairs={{16,0},{32,16},{48,32},{64,48},{80,64},{96,80},{112,96},{128,112},... | collective-permute-start | bytes 208904 | tf_op jit(solution)/shard_map/ppermute | solution.py:18
  100.8 43.6 %copy-start.2 = (f32[17,4,8,128]{3,2,1,0:T(8,128)S(1)}, f32[17,4,8,128]{3,2,1,0:T(8,128)}, u32[]{:S(2)}) copy-start(f32[17,4,8,128]{3,2,1,0:T(8,128)} %param.7) | copy-start | bytes 835588
  100.8 43.6 %copy-start.8 = (f32[17]{0:T(128)S(1)}, f32[17]{0:T(128)}, u32[]{:S(2)}) copy-start(f32[17]{0:T(128)} %copy-done.6) | copy-start | bytes 208
  144.6 8.7 %collective-permute-start.8 = (f32[17,1,8,128]{3,2,1,0:T(8,128)S(1)}, f32[17,1,8,128]{3,2,1,0:T(8,128)S(1)}, u32[]{:S(2)}, u32[]{:S(2)}) collective-permute-start(f32[17,1,8,128]{3,2,1,0:T(8,128)S(1)} %slice.144), channel_id=1, source_target_pairs={{0,16},{16,32},{32,48},{48,64},{64,80},{80,96},{96,112},{112,128},... | collective-permute-start | bytes 208904 | tf_op jit(solution)/shard_map/ppermute | solution.py:44
  153.3 5.6 %collective-permute-start.9 = (f32[17,2,1,128]{3,2,1,0:T(1,128)S(1)}, f32[17,2,1,128]{3,2,1,0:T(1,128)S(1)}, u32[]{:S(2)}, u32[]{:S(2)}) collective-permute-start(f32[17,2,1,128]{3,2,1,0:T(1,128)S(1)} %slice.146), channel_id=1, source_target_pairs={{0,4},{4,8},{8,12},{1,5},{5,9},{9,13},{2,6},{6,10},{10,14},{3,7},{... | collective-permute-start | bytes 52232 | tf_op jit(solution)/shard_map/ppermute | solution.py:44
where the time goes:
time: 166 us; the launch traced here: 165 us
  waiting for transfers between devices  51.4 us (31%)
  blocking collectives  43.4 us (26%)
  starting transfers between devices  42.8 us (26%)
  local copies, waits for them, and re-layouts  12.9 us (8%)
  other arithmetic  8.98 us (5%)
  matrix products  4.49 us (3%)
    all_to_all x1, blocking collectives, sum_at_owner(): lax.all_to_all(pieces, axis, split_axis=0, concat_axis=0, tiled=True)  43.4 us
    all_to_all x1, waiting for transfers between devices, sum_at_owner(): lax.all_to_all(pieces, axis, split_axis=0, concat_axis=0, tiled=True)  40.7 us
    ppermute x4, starting transfers between devices, padded_2(): lax.ppermute(initial, axis, [(b, a) for a, b in up])  19.7 us
    ppermute x4, starting transfers between devices, padded_2(): lax.ppermute(last, axis, up)  13.2 us
    ppermute x2, waiting for transfers between devices, shifted(): return lax.ppermute(array, axis, pairs)  8.97 us
    all_to_all x1, starting transfers between devices, sum_at_owner(): lax.all_to_all(pieces, axis, split_axis=0, concat_axis=0, tiled=True)  5.43 us
    mul x2, local copies, waits for them, and re-layouts, operate(): scaled = (var_coefs[:, None] * lap[None]).reshape(terms * slots, cells)  5.43 us
    dot_general x2, matrix products, operate(): jnp.dot(col_table, scaled, precision=lax.Precision.HIGHEST)  4.49 us
  transfers between devices with their start and end apart: 11, of which 5 were waited for; matrix products, arithmetic and copies ran while one was open for 2% of the time, Pallas kernels for 0%

commit v1 on v0

v1 whole, which is shorter than its diff:
```python
import jax
import jax.numpy as jnp
from jax import lax
from jax.experimental import pallas as pl
from jax.experimental.pallas import tpu as pltpu
from jax.sharding import PartitionSpec as P


P_SIZE = 66
MESH = pl.DeviceIdType.MESH
SL = 17
OWN = 136
VEC = 72
ALL = 8 * VEC
TERMS = 10
KSEG = 80
F32 = jnp.float32
BF16 = jnp.bfloat16


def lanes(rows):
    return lax.broadcasted_iota(jnp.int32, (rows, 128), 1)


def swing(a):
    return pltpu.roll(a, 64, 1)


def kernel(
    field, source, mean, var, cols, vals, smoothed, coarse,
    fs, ss, cs, fr, sr, cr, v1, v2, xlo1, xhi1, ylo1, yhi1, z1, xlo2, xhi2, ylo2, yhi2, z2,
    ysend1, ysend2, lap, rhs, left, left16, gt, gt2, srcv, after, wz, bs, br, dbuf, cxs, cys, cxr, cyr, cxyr, fin, cbs, cbr,
    send, recv,
):
    gx, gy, ch = lax.axis_index("gx"), lax.axis_index("gy"), lax.axis_index("chaos")
    hi, core = ch // 2, ch % 2
    chip = hi * 4 + gy
    pos = (chip + 6) % 8
    side, blk = pos // 4, pos % 4
    xi = gx * 2 + core
    last_x = 2 * lax.axis_size("gx") - 1

    far_gy = (gy + 2) % 4

    def worker(s, c):
        return (gx, far_gy, (((gy + 2 + 4 * s) % 8) // 4) * 2 + c)

    def owner(j):
        return (gx, far_gy, j)

    def place(dx, dy):
        x, d = xi + dx, (chip + dy + 8) % 8
        return (x // 2, d % 4, (d // 4) * 2 + x % 2)

    has_xp, has_xn = xi > 0, xi < last_x
    has_yp, has_yn = blk > 0, blk < 3
    across = (gx, gy, (1 - hi) * 2 + core)

    barrier = pltpu.get_barrier_semaphore()
    neighbours = [
        (has_xp, place(-1, 0)), (has_xn, place(1, 0)), (has_yp, place(0, -1)), (has_yn, place(0, 1)),
        (jnp.logical_and(has_xp, has_yp), place(-1, -1)), (jnp.logical_and(has_xn, has_yn), place(1, 1)),
    ]
    for j in range(4):
        pl.semaphore_signal(barrier, inc=1, device_id=owner(j), device_id_type=MESH)
    pl.semaphore_signal(barrier, inc=1, device_id=across, device_id_type=MESH)
    for cond, dev in neighbours:
        @pl.when(cond)
        def _():
            pl.semaphore_signal(barrier, inc=1, device_id=dev, device_id_type=MESH)

    keep = (lax.broadcasted_iota(jnp.int32, (16, 128), 0) + SL * ch < P_SIZE)
    keep_tail = SL * ch + 16 < P_SIZE
    low16, low8 = lanes(16) < 64, lanes(8) < 64

    def tails(t):
        r = pltpu.roll(swing(t), 4, 0)
        return jnp.where(low8, t, r), swing(jnp.where(low8, r, t))

    def pack(ref, out):
        for x in range(4):
            c, xl = x // 2, x % 2
            for y in range(4):
                v = xl * 4 + y
                a = jnp.where(keep, ref[pl.ds(x * 8 + y, 16, stride=32), :], 0.0)
                b = swing(jnp.where(keep, ref[pl.ds(x * 8 + y + 4, 16, stride=32), :], 0.0))
                out[pl.ds(c * OWN + v * 16, 16), :] = jnp.where(low16, a, b)
                out[pl.ds((2 + c) * OWN + v * 16, 16), :] = swing(jnp.where(low16, b, a))
            ta, tb = tails(jnp.where(keep_tail, ref[pl.ds(512 + x * 8, 8), :], 0.0))
            out[pl.ds(c * OWN + 128 + xl * 4, 4), :] = ta[0:4]
            out[pl.ds((2 + c) * OWN + 128 + xl * 4, 4), :] = tb[0:4]

    def piece(ref, i):
        return ref.at[pl.ds(pl.multiple_of(i * OWN, 8), OWN), :]

    def copy(src, dst, k, l, dev):
        return pltpu.make_async_remote_copy(
            src_ref=src, dst_ref=dst, send_sem=send.at[k], recv_sem=recv.at[l], device_id=dev, device_id_type=MESH
        )

    pack(field, fs)
    pl.semaphore_wait(barrier, 5 + sum(jnp.where(cond, 1, 0) for cond, dev in neighbours))

    for c in range(2):
        for s in range(2):
            copy(piece(fs, 2 * s + c), piece(fr, ch), 2 * s + c, ch, worker(s, c)).start()

    for k in range(TERMS + 1):
        for xl in range(2):
            if k < TERMS:
                t = var[pl.ds(pl.multiple_of(k * 32 + core * 16 + xl * 8, 8), 8), :]
            else:
                t = mean[pl.ds(pl.multiple_of(core * 16 + xl * 8, 8), 8), :]
            ta, tb = tails(t)
            cs[pl.ds(k * 8 + xl * 4, 4), :] = jnp.where(hi == 0, ta, tb)[0:4]
    coefs = copy(cs, cr, 8, 8, worker(hi, core))
    coefs.start()

    pack(source, ss)
    for c in range(2):
        for s in range(2):
            copy(piece(ss, 2 * s + c), piece(sr, ch), 4 + 2 * s + c, 4 + ch, worker(s, c)).start()

    zero_vec = jnp.zeros((VEC, 128), F32)
    for cond, xref, yref in ((xi == 0, (xlo1, xlo2), ()), (xi == last_x, (xhi1, xhi2), ()),
                             (blk == 0, (), (ylo1, ylo2)), (blk == 3, (), (yhi1, yhi2))):
        @pl.when(cond)
        def _():
            for ref in xref:
                for i in range(4):
                    ref[pl.ds(i * VEC, VEC), :] = zero_vec
            for ref in yref:
                ref[...] = zero_vec

    @pl.when(xi == 0)
    def _():
        cxr[...] = jnp.zeros((2 * VEC, 128), F32)

    @pl.when(blk == 0)
    def _():
        cyr[...] = zero_vec

    @pl.when(jnp.logical_or(xi == 0, blk == 0))
    def _():
        cxyr[...] = zero_vec

    rhs[...] = jnp.zeros((4 * 256, 256), BF16)
    gt[...] = jnp.zeros((128, 128), F32)
    p = lax.broadcasted_iota(jnp.int32, (KSEG, 68), 0)
    slot = jnp.where(p < 64, SL * lax.shift_right_logical(p, 4) + jnp.bitwise_and(p, 15),
                     jnp.where(p < 68, SL * (p - 64) + 16, -1))
    used = lax.broadcasted_iota(jnp.int32, (1, 68), 1) < P_SIZE
    lane72 = lanes(VEC)

    def build(k, carry):
        total = jnp.zeros((KSEG, 68), F32)
        for b in range(3):
            total = total + jnp.where(slot == cols[k, b:b + 1, :], jnp.where(used, vals[k, b:b + 1, :], 0.0), 0.0)
        gt[0:KSEG, 0:68] = total
        gt2[...] = jnp.transpose(gt[...])
        rows = [gt2[pl.ds(SL * j, 16), :] for j in range(4)]
        rows.append(gt2[pl.ds(16, 4, stride=SL), :])
        rows.append(jnp.zeros((4, 128), F32))
        g = jnp.concatenate(rows, 0)
        a1 = g.astype(BF16).astype(F32)
        a2 = g - a1
        r = pltpu.roll(a1, KSEG, 1)
        left[pl.ds(pl.multiple_of(k * VEC, 8), VEC), 0:128] = jnp.where(lane72 < 80, a1, r)
        left[pl.ds(pl.multiple_of(k * VEC, 8), VEC), 128:256] = jnp.where(lane72 < 32, r, pltpu.roll(a2, 32, 1))
        return carry

    lax.fori_loop(0, TERMS, build, 0)
    left16[...] = left[...].astype(BF16)

    row = lax.broadcasted_iota(jnp.int32, (256, 256), 0)
    col = lax.broadcasted_iota(jnp.int32, (256, 256), 1)
    half = jnp.bitwise_and(lax.shift_right_logical(row, 6), 1)
    b_row = 2 * half + lax.shift_right_logical(row, 7)
    z_row = jnp.bitwise_and(row, 63)
    off = z_row - 2 * jnp.bitwise_and(col, 31)
    near = jnp.where(off == 0, 0.5, jnp.where(jnp.logical_or(off == 1, off == -1), 0.25, 0.0))
    main_w = jnp.where(jnp.logical_and(col < 128, lax.shift_right_logical(col, 5) == b_row), near, 0.0)
    next_w = jnp.where(jnp.logical_and(col == 128 + b_row, z_row == 63), 0.25, 0.0)
    wz[...] = (main_w + next_w).astype(BF16)

    low = lane72 < 64
    z64 = jnp.bitwise_and(lane72, 63)
    edge = 63 * (1 - side)
    edge_lane = z64 == edge
    first_lane, end_lane = z64 == 0, z64 == 63

    def vec(ref, v):
        return ref[pl.ds(v * VEC, VEC), :]

    def gather(src, dst):
        for v in range(8):
            for j in range(4):
                dst[pl.ds(v * VEC + 16 * j, 16), :] = src[pl.ds(j * OWN + 16 * v, 16), :]
            dst[pl.ds(v * VEC + 64, 4), :] = src[pl.ds(128 + v, 4, stride=OWN), :]
            dst[pl.ds(v * VEC + 68, 4), :] = jnp.zeros((4, 128), F32)

    def arrived(dst, k, l):
        copy(dst, dst, k, l, across).wait_recv()

    def spread(val, stage, halos, base):
        xlo, xhi, ylo, yhi, z = halos
        up = stage.at[pl.ds(0, VEC), :]
        down = stage.at[pl.ds(VEC, VEC), :]
        zs = stage.at[pl.ds(2 * VEC, VEC), :]
        xn = copy(val.at[pl.ds(4 * VEC, 4 * VEC), :], xlo, base, base, place(1, 0))
        xp = copy(val.at[pl.ds(0, 4 * VEC), :], xhi, base + 1, base + 1, place(-1, 0))
        yn = copy(up, ylo, base + 2, base + 2, place(0, 1))
        yp = copy(down, yhi, base + 3, base + 3, place(0, -1))
        zc = copy(zs, z, base + 4, base + 4, across)

        total = zero_vec
        for v in range(8):
            total = jnp.where(z64 == v, pltpu.roll(vec(val, v), v + 65 * (1 - side), 1), total)
        zs[...] = total
        zc.start()

        @pl.when(has_xn)
        def _():
            xn.start()

        @pl.when(has_xp)
        def _():
            xp.start()

        up[...] = jnp.where(low, swing(vec(val, 3)), vec(val, 7))
        down[...] = jnp.where(low, vec(val, 0), swing(vec(val, 4)))

        @pl.when(has_yn)
        def _():
            yn.start()

        @pl.when(has_yp)
        def _():
            yp.start()

        return xn, xp, yn, yp, zc

    def collect(ops):
        xn, xp, yn, yp, zc = ops

        @pl.when(has_xp)
        def _():
            xn.wait_recv()

        @pl.when(has_xn)
        def _():
            xp.wait_recv()

        @pl.when(has_yp)
        def _():
            yn.wait_recv()

        @pl.when(has_yn)
        def _():
            yp.wait_recv()

        zc.wait_recv()

    def laplace(val, halos):
        xlo, xhi, ylo, yhi, z = halos
        for x in range(2):
            for y in range(4):
                v = 4 * x + y
                here = vec(val, v)
                beside = (vec(val, v - 4) if x else vec(xlo, y)) + (vec(xhi, y) if x else vec(val, v + 4))
                if y > 0:
                    beside = beside + vec(val, v - 1)
                elif x == 0:
                    beside = beside + jnp.where(low, ylo[...], swing(vec(val, 3)))
                else:
                    beside = beside + swing(jnp.where(low, vec(val, 7), ylo[...]))
                if y < 3:
                    beside = beside + vec(val, v + 1)
                elif x == 0:
                    beside = beside + swing(jnp.where(low, yhi[...], vec(val, 0)))
                else:
                    beside = beside + jnp.where(low, swing(vec(val, 4)), yhi[...])
                beside = beside + jnp.where(first_lane, 0.0, pltpu.roll(here, 1, 1))
                beside = beside + jnp.where(end_lane, 0.0, pltpu.roll(here, 127, 1))
                beside = beside + jnp.where(edge_lane, pltpu.roll(z[...], (edge + 128 - v) % 128, 1), 0.0)
                out = 6.0 * here - beside
                lap[pl.ds(v * VEC, VEC), :] = out
                b1 = out.astype(BF16)
                b2 = (out - b1.astype(F32)).astype(BF16)
                r, h = (v // 2) * 256, (v % 2) * 128
                rhs[r:r + VEC, h:h + 128] = b1
                rhs[r + KSEG:r + KSEG + VEC, h:h + 128] = b2
                rhs[r + 2 * KSEG:r + 2 * KSEG + VEC, h:h + 128] = b1

    def operate(use):
        def step(q, carry):
            mixed = jnp.dot(
                left16[...], rhs[pl.ds(pl.multiple_of(q * 256, 256), 256), :], preferred_element_type=F32
            )
            for h in range(2):
                v = 2 * q + h
                rows = pl.ds(pl.multiple_of(v * VEC, 8), VEC)
                m = cr[pl.ds(TERMS * 8 + v, 1), :]
                total = m * lap[rows, :]
                for k in range(TERMS):
                    total = total + cr[pl.ds(k * 8 + v, 1), :] * mixed[k * VEC:(k + 1) * VEC, h * 128:(h + 1) * 128]
                use(rows, m, total)
            return carry

        lax.fori_loop(0, 4, step, 0)

    for j in range(4):
        arrived(piece(fr, j), j, j)
    gather(fr, v1)
    halos1 = (xlo1, xhi1, ylo1, yhi1, z1)
    ops1 = spread(v1, ysend1, halos1, 9)
    arrived(cr, 8, 8)
    collect(ops1)
    laplace(v1, halos1)
    for j in range(4):
        arrived(piece(sr, j), 4 + j, 4 + j)
    gather(sr, srcv)

    def relax(rows, m, total):
        first = srcv[rows, :] - total
        v2[rows, :] = v1[rows, :] + (2.0 / 3.0) * first / (6.0 * m)

    operate(relax)

    halos2 = (xlo2, xhi2, ylo2, yhi2, z2)
    ops2 = spread(v2, ysend2, halos2, 14)
    for j in range(4):
        for v in range(8):
            bs[pl.ds(j * OWN + 16 * v, 16), :] = v2[pl.ds(v * VEC + 16 * j, 16), :]
        bs[pl.ds(j * OWN + 128, 8), :] = v2[pl.ds(64 + j, 8, stride=VEC), :]
    here = 2 * side + core
    for j in range(4):
        copy(piece(bs, j), piece(br, here), 19 + j, 19 + here, owner(j)).start()
    collect(ops2)
    laplace(v2, halos2)

    def residual(rows, m, total):
        after[rows, :] = srcv[rows, :] - total

    operate(residual)

    for i in range(2):
        if i == 0:
            c = [0.5 * vec(after, y) + 0.25 * vec(after, 4 + y) for y in range(4)]
        else:
            c = [0.25 * vec(after, 4 + y) for y in range(4)]
        s3 = 0.25 * swing(c[3])
        d0 = 0.5 * c[0] + 0.25 * c[1] + jnp.where(low, 0.0, s3)
        d1 = 0.5 * c[2] + 0.25 * (c[3] + c[1])
        dn = jnp.where(low, s3, 0.0)
        for r, (da, db) in ((i, (d0, d1)), (2 + i, (dn, None))):
            for h, d in ((0, da), (1, db)):
                if d is None:
                    d = zero_vec
                dh = d.astype(BF16)
                dbuf[pl.ds(r * VEC, VEC), h * 128:(h + 1) * 128] = dh.astype(F32)
                dbuf[pl.ds((4 + r) * VEC, VEC), h * 128:(h + 1) * 128] = d - dh.astype(F32)
    parts = jnp.dot(dbuf[...].astype(BF16), wz[...], preferred_element_type=F32)
    parts = parts[0:4 * VEC] + parts[4 * VEC:8 * VEC]

    def both(r):
        return parts[r * VEC:(r + 1) * VEC, 0:128], parts[r * VEC:(r + 1) * VEC, 128:256]

    def one(r):
        a, b = both(r)
        return a + pltpu.roll(b, 32, 1)

    a, b = both(1)
    cxs[0:VEC, :] = a
    cxs[VEC:2 * VEC, :] = b
    cx = copy(cxs, cxr, 23, 23, place(1, 0))

    @pl.when(has_xn)
    def _():
        cx.start()

    cys[0:VEC, :] = one(2)
    cys[VEC:2 * VEC, :] = one(3)
    cy = copy(cys.at[pl.ds(0, VEC), :], cyr, 24, 24, place(0, 1))
    cxy = copy(cys.at[pl.ds(VEC, VEC), :], cxyr, 25, 25, place(1, 1))

    @pl.when(has_yn)
    def _():
        cy.start()

    @pl.when(jnp.logical_and(has_xn, has_yn))
    def _():
        cxy.start()

    for j in range(4):
        arrived(piece(br, j), 19 + j, 19 + j)
    for x in range(4):
        c, xl = x // 2, x % 2
        for y in range(4):
            v = 4 * xl + y
            va = br[pl.ds(c * OWN + 16 * v, 16), :]
            vb = br[pl.ds((2 + c) * OWN + 16 * v, 16), :]
            smoothed[pl.ds(x * 8 + y, 16, stride=32), :] = jnp.where(low16, va, swing(vb))
            smoothed[pl.ds(x * 8 + y + 4, 16, stride=32), :] = jnp.where(low16, swing(va), vb)
        ta = br[pl.ds(c * OWN + 128, 8), :]
        tb = br[pl.ds((2 + c) * OWN + 128, 8), :]
        smoothed[pl.ds(512 + x * 8, 4), :] = jnp.where(low8, ta, swing(tb))[4 * xl:4 * xl + 4]
        smoothed[pl.ds(512 + x * 8 + 4, 4), :] = jnp.where(low8, swing(ta), tb)[4 * xl:4 * xl + 4]

    a, b = both(0)

    @pl.when(has_xp)
    def _():
        cx.wait_recv()

    @pl.when(has_yp)
    def _():
        cy.wait_recv()

    @pl.when(jnp.logical_and(has_xp, has_yp))
    def _():
        cxy.wait_recv()

    ysum = cyr[...] + cxyr[...]
    fin[0:VEC, :] = a + cxr[0:VEC, :] + jnp.where(lane72 < 32, ysum, 0.0)
    fin[VEC:2 * VEC, :] = b + cxr[VEC:2 * VEC, :] + jnp.where(lane72 == 0, pltpu.roll(ysum, 96, 1), 0.0)
    for j in range(4):
        cbs[pl.ds(j * 40, 16), :] = fin[pl.ds(16 * j, 16), :]
        cbs[pl.ds(j * 40 + 16, 16), :] = fin[pl.ds(VEC + 16 * j, 16), :]
        cbs[pl.ds(j * 40 + 32, 2), :] = fin[pl.ds(64 + j, 2, stride=VEC), :]
        cbs[pl.ds(j * 40 + 34, 6), :] = jnp.zeros((6, 128), F32)

    def small(ref, i):
        return ref.at[pl.ds(pl.multiple_of(i * 40, 8), 40), :]

    for j in range(4):
        copy(small(cbs, j), small(cbr, here), 26 + j, 26 + here, owner(j)).start()
    for j in range(4):
        arrived(small(cbr, j), 26 + j, 26 + j)
    lane16 = lanes(16)
    for x in range(2):
        ma, mb = cbr[pl.ds(x * 40, 16), :], cbr[pl.ds((2 + x) * 40, 16), :]
        za = cbr[pl.ds(x * 40 + 16, 16), :]
        tl, tr = cbr[pl.ds(x * 40 + 32, 8), :], cbr[pl.ds((2 + x) * 40 + 32, 8), :]
        for b in range(4):
            def joined(left_, right_, extra, lane):
                out = jnp.where(lane < 32, pltpu.roll(left_, (128 - 32 * b) % 128, 1), pltpu.roll(right_, (160 - 32 * b) % 128, 1))
                return out + jnp.where(lane == 32, pltpu.roll(extra, 32 - b, 1), 0.0)

            coarse[pl.ds(x * 4 + b, 16, stride=8), :] = joined(ma, mb, za, lane16)
            t = joined(tl, tr, pltpu.roll(tl, 7, 0), lanes(8))
            coarse[pl.ds(128 + x * 4 + b, 1), :] = t[0:1]

    for j in range(4):
        copy(piece(fs, j), piece(fr, j), j, j, across).wait_send()
        copy(piece(ss, j), piece(sr, j), 4 + j, 4 + j, across).wait_send()
        copy(piece(bs, j), piece(br, j), 19 + j, 19 + j, across).wait_send()
        copy(small(cbs, j), small(cbr, j), 26 + j, 26 + j, across).wait_send()
    coefs.wait_send()
    for xn, xp, yn, yp, zc in (ops1, ops2):
        zc.wait_send()
        for cond, op in ((has_xn, xn), (has_xp, xp), (has_yn, yn), (has_yp, yp)):
            @pl.when(cond)
            def _():
                op.wait_send()
    for cond, op in ((has_xn, cx), (has_yn, cy), (jnp.logical_and(has_xn, has_yn), cxy)):
        @pl.when(cond)
        def _():
            op.wait_send()


def scratch():
    def rows(n, width=128, kind=F32):
        return pltpu.VMEM((n, width), kind)

    halos = [rows(4 * VEC), rows(4 * VEC), rows(VEC), rows(VEC), rows(VEC)]
    return [
        rows(4 * OWN), rows(4 * OWN), rows(8 * (TERMS + 1)), rows(4 * OWN), rows(4 * OWN), rows(8 * (TERMS + 1)),
        rows(ALL), rows(ALL), *halos, *halos, rows(3 * VEC), rows(3 * VEC), rows(ALL), rows(4 * 256, 256, BF16),
        rows(TERMS * VEC, 256), rows(TERMS * VEC, 256, BF16), rows(128), rows(128), rows(ALL), rows(ALL), rows(256, 256, BF16),
        rows(4 * OWN), rows(4 * OWN), rows(8 * VEC, 256), rows(2 * VEC), rows(2 * VEC), rows(2 * VEC), rows(VEC),
        rows(VEC), rows(2 * VEC), rows(160), rows(160),
        pltpu.SemaphoreType.DMA((30,)), pltpu.SemaphoreType.DMA((30,)),
    ]


def body(field, source, mean_coef, var_coefs, galerkin_cols, galerkin_vals):
    whole = pl.BlockSpec(memory_space=pltpu.VMEM)
    smoothed, coarse = pl.pallas_call(
        kernel,
        out_shape=(jax.ShapeDtypeStruct((SL * 32, 128), F32), jax.ShapeDtypeStruct((SL * 8, 128), F32)),
        in_specs=[whole] * 6,
        out_specs=(whole, whole),
        scratch_shapes=scratch(),
        compiler_params=pltpu.CompilerParams(collective_id=0, has_side_effects=True),
        name="sweep",
    )(
        field.reshape(SL * 32, 128), source.reshape(SL * 32, 128), mean_coef.reshape(32, 128),
        var_coefs.reshape(TERMS * 32, 128), jnp.swapaxes(galerkin_cols, 1, 2), jnp.swapaxes(galerkin_vals, 1, 2),
    )
    return smoothed.reshape(field.shape), coarse[:, 0:64].reshape(SL, 2, 4, 64)


def solution(mesh):
    wide = P("chaos", "gx", "gy", None)
    return jax.shard_map(
        body,
        mesh=mesh,
        in_specs=(wide, wide, P("gx", "gy", None), P(None, "gx", "gy", None), P(), P()),
        out_specs=(wide, wide),
        check_vma=False,
    )
```

time: 166 us -> 54.3 us (0.33)
  the two profiles are of different devices: /device:TPU:22 before, /device:TPU:23 now
where the time goes in v1:
time: 54.3 us; the launch traced here: 54.2 us
  Pallas kernels  51.2 us (94%)
  local copies, waits for them, and re-layouts  2.35 us (4%)
  between operations  0.65 us (1%)
    pallas_call x1, Pallas kernels, body(): pl.pallas_call(kernel, out_shape=(jax.ShapeDtypeStruct((SL * 32, 128), F3...  51.2 us
    unnamed x4, local copies, waits for them, and re-layouts  2.35 us

profile of v1, /device:TPU:23, one launch (start us, length us, event | category | flops | bytes accessed | tf_op | source)
XLA Modules:
  0.0 54.2 jit_solution(262866504843334553)
XLA Ops:
  0.6 51.2 %sweep.1 = (f32[544,128]{1,0:T(8,128)}, f32[136,128]{1,0:T(8,128)}) custom-call(f32[544,128]{1,0:T(8,128)} %bitcast.9, f32[544,128]{1,0:T(8,128)} %bitcast.10, f32[32,128]{1,0:T(8,128)} %bitcast.16, f32[320,128]{1,0:T(8,128)} %bitcast.12, s32[10,3,68]{2,1,0:T(4,128)} %bitcast.14, f32[10,3,68]{2,1,0:T(4,128)} %bitcast.15), custom_call_target="tpu_custom_call" | custom-call | tf_op jit(solution)/shard_map/sweep/pallas_call | solution.py:489
  51.8 0.0 copy-start
  51.8 1.7 %copy.10 = f32[17,4,8,128]{3,2,1,0:T(8,128)} copy(f32[17,4,8,128]{3,2,1,0:T(8,128)} %bitcast.11) | data formatting | bytes 557056
  53.5 0.0 copy-done
  53.5 0.6 %copy.11 = f32[17,2,4,64]{3,2,1,0:T(4,128)} copy(f32[17,2,4,64]{3,2,1,0:T(4,128)S(1)} %bitcast.13) | data formatting | bytes 69632
Async XLA Ops:
  51.8 1.7 %copy-start = (f32[136,128]{1,0:T(8,128)S(1)}, f32[136,128]{1,0:T(8,128)}, u32[]{:S(2)}) copy-start(f32[136,128]{1,0:T(8,128)} %get-tuple-element.5) | copy-start | bytes 208900

commit v2 on v1

--- a/solution.py
+++ b/solution.py
@@ -27,8 +27,9 @@
 
 
 def kernel(
-    field, source, mean, var, cols, vals, smoothed, coarse,
-    fs, ss, cs, fr, sr, cr, v1, v2, xlo1, xhi1, ylo1, yhi1, z1, xlo2, xhi2, ylo2, yhi2, z2,
+    field_in, source_in, mean_in, var_in, cols_in, vals_in, smoothed, coarse,
+    field, source, mean, var, cols, vals, loads,
+    fs, ss, cs, fr, sr, cr, v1, v2, xlo1, xhi1, ylo1, yhi1, z1, xlo2, xhi2, ylo2, yhi2, z2, zfull,
     ysend1, ysend2, lap, rhs, left, left16, gt, gt2, srcv, after, wz, bs, br, dbuf, cxs, cys, cxr, cyr, cxyr, fin, cbs, cbr,
     send, recv,
 ):
@@ -68,6 +69,13 @@
         @pl.when(cond)
         def _():
             pl.semaphore_signal(barrier, inc=1, device_id=dev, device_id_type=MESH)
+
+    pairs = (
+        (field_in, field), (var_in, var), (mean_in, mean), (source_in, source), (cols_in, cols), (vals_in, vals),
+    )
+    staged = [pltpu.make_async_copy(a, b, loads.at[i]) for i, (a, b) in enumerate(pairs)]
+    for op in staged:
+        op.start()
 
     keep = (lax.broadcasted_iota(jnp.int32, (16, 128), 0) + SL * ch < P_SIZE)
     keep_tail = SL * ch + 16 < P_SIZE
@@ -98,6 +106,7 @@
             src_ref=src, dst_ref=dst, send_sem=send.at[k], recv_sem=recv.at[l], device_id=dev, device_id_type=MESH
         )
 
+    staged[0].wait()
     pack(field, fs)
     pl.semaphore_wait(barrier, 5 + sum(jnp.where(cond, 1, 0) for cond, dev in neighbours))
 
@@ -105,6 +114,8 @@
         for s in range(2):
             copy(piece(fs, 2 * s + c), piece(fr, ch), 2 * s + c, ch, worker(s, c)).start()
 
+    staged[1].wait()
+    staged[2].wait()
     for k in range(TERMS + 1):
         for xl in range(2):
             if k < TERMS:
@@ -116,6 +127,7 @@
     coefs = copy(cs, cr, 8, 8, worker(hi, core))
     coefs.start()
 
+    staged[3].wait()
     pack(source, ss)
     for c in range(2):
         for s in range(2):
@@ -144,45 +156,7 @@
     def _():
         cxyr[...] = zero_vec
 
-    rhs[...] = jnp.zeros((4 * 256, 256), BF16)
-    gt[...] = jnp.zeros((128, 128), F32)
-    p = lax.broadcasted_iota(jnp.int32, (KSEG, 68), 0)
-    slot = jnp.where(p < 64, SL * lax.shift_right_logical(p, 4) + jnp.bitwise_and(p, 15),
-                     jnp.where(p < 68, SL * (p - 64) + 16, -1))
-    used = lax.broadcasted_iota(jnp.int32, (1, 68), 1) < P_SIZE
     lane72 = lanes(VEC)
-
-    def build(k, carry):
-        total = jnp.zeros((KSEG, 68), F32)
-        for b in range(3):
-            total = total + jnp.where(slot == cols[k, b:b + 1, :], jnp.where(used, vals[k, b:b + 1, :], 0.0), 0.0)
-        gt[0:KSEG, 0:68] = total
-        gt2[...] = jnp.transpose(gt[...])
-        rows = [gt2[pl.ds(SL * j, 16), :] for j in range(4)]
-        rows.append(gt2[pl.ds(16, 4, stride=SL), :])
-        rows.append(jnp.zeros((4, 128), F32))
-        g = jnp.concatenate(rows, 0)
-        a1 = g.astype(BF16).astype(F32)
-        a2 = g - a1
-        r = pltpu.roll(a1, KSEG, 1)
-        left[pl.ds(pl.multiple_of(k * VEC, 8), VEC), 0:128] = jnp.where(lane72 < 80, a1, r)
-        left[pl.ds(pl.multiple_of(k * VEC, 8), VEC), 128:256] = jnp.where(lane72 < 32, r, pltpu.roll(a2, 32, 1))
-        return carry
-
-    lax.fori_loop(0, TERMS, build, 0)
-    left16[...] = left[...].astype(BF16)
-
-    row = lax.broadcasted_iota(jnp.int32, (256, 256), 0)
-    col = lax.broadcasted_iota(jnp.int32, (256, 256), 1)
-    half = jnp.bitwise_and(lax.shift_right_logical(row, 6), 1)
-    b_row = 2 * half + lax.shift_right_logical(row, 7)
-    z_row = jnp.bitwise_and(row, 63)
-    off = z_row - 2 * jnp.bitwise_and(col, 31)
-    near = jnp.where(off == 0, 0.5, jnp.where(jnp.logical_or(off == 1, off == -1), 0.25, 0.0))
-    main_w = jnp.where(jnp.logical_and(col < 128, lax.shift_right_logical(col, 5) == b_row), near, 0.0)
-    next_w = jnp.where(jnp.logical_and(col == 128 + b_row, z_row == 63), 0.25, 0.0)
-    wz[...] = (main_w + next_w).astype(BF16)
-
     low = lane72 < 64
     z64 = jnp.bitwise_and(lane72, 63)
     edge = 63 * (1 - side)
@@ -203,10 +177,10 @@
         copy(dst, dst, k, l, across).wait_recv()
 
     def spread(val, stage, halos, base):
-        xlo, xhi, ylo, yhi, z = halos
+        xlo, xhi, ylo, yhi, z, zfull = halos
         up = stage.at[pl.ds(0, VEC), :]
         down = stage.at[pl.ds(VEC, VEC), :]
-        zs = stage.at[pl.ds(2 * VEC, VEC), :]
+        zs = stage.at[pl.ds(2 * VEC, 16), :]
         xn = copy(val.at[pl.ds(4 * VEC, 4 * VEC), :], xlo, base, base, place(1, 0))
         xp = copy(val.at[pl.ds(0, 4 * VEC), :], xhi, base + 1, base + 1, place(-1, 0))
         yn = copy(up, ylo, base + 2, base + 2, place(0, 1))
@@ -216,7 +190,11 @@
         total = zero_vec
         for v in range(8):
             total = jnp.where(z64 == v, pltpu.roll(vec(val, v), v + 65 * (1 - side), 1), total)
-        zs[...] = total
+        for t in range(8):
+            part = total[8 * t:8 * t + 8]
+            packed = jnp.where(z64[0:8] // 8 == t, pltpu.roll(part, 8 * t, 1) if t else part, packed) if t else part
+        stage[pl.ds(2 * VEC, 8), :] = packed
+        stage[pl.ds(2 * VEC + 8, 8), :] = total[64:72]
         zc.start()
 
         @pl.when(has_xn)
@@ -262,7 +240,10 @@
         zc.wait_recv()
 
     def laplace(val, halos):
-        xlo, xhi, ylo, yhi, z = halos
+        xlo, xhi, ylo, yhi, zpacked, z = halos
+        for t in range(8):
+            z[pl.ds(8 * t, 8), :] = pltpu.roll(zpacked[0:8, :], (128 - 8 * t) % 128, 1) if t else zpacked[0:8, :]
+        z[pl.ds(64, 8), :] = zpacked[8:16, :]
         for x in range(2):
             for y in range(4):
                 v = 4 * x + y
@@ -312,8 +293,37 @@
     for j in range(4):
         arrived(piece(fr, j), j, j)
     gather(fr, v1)
-    halos1 = (xlo1, xhi1, ylo1, yhi1, z1)
+    halos1 = (xlo1, xhi1, ylo1, yhi1, z1, zfull)
     ops1 = spread(v1, ysend1, halos1, 9)
+    rhs[...] = jnp.zeros((4 * 256, 256), BF16)
+    gt[...] = jnp.zeros((128, 128), F32)
+    staged[4].wait()
+    staged[5].wait()
+    p = lax.broadcasted_iota(jnp.int32, (KSEG, 68), 0)
+    slot = jnp.where(p < 64, SL * lax.shift_right_logical(p, 4) + jnp.bitwise_and(p, 15),
+                     jnp.where(p < 68, SL * (p - 64) + 16, -1))
+    used = lax.broadcasted_iota(jnp.int32, (1, 68), 1) < P_SIZE
+
+    def build(k, carry):
+        total = jnp.zeros((KSEG, 68), F32)
+        for b in range(3):
+            total = total + jnp.where(slot == cols[k, b:b + 1, :], jnp.where(used, vals[k, b:b + 1, :], 0.0), 0.0)
+        gt[0:KSEG, 0:68] = total
+        gt2[...] = jnp.transpose(gt[...])
+        rows = [gt2[pl.ds(SL * j, 16), :] for j in range(4)]
+        rows.append(gt2[pl.ds(16, 4, stride=SL), :])
+        rows.append(jnp.zeros((4, 128), F32))
+        g = jnp.concatenate(rows, 0)
+        a1 = g.astype(BF16).astype(F32)
+        a2 = g - a1
+        r = pltpu.roll(a1, KSEG, 1)
+        left[pl.ds(pl.multiple_of(k * VEC, 8), VEC), 0:128] = jnp.where(lane72 < 80, a1, r)
+        left[pl.ds(pl.multiple_of(k * VEC, 8), VEC), 128:256] = jnp.where(lane72 < 32, r, pltpu.roll(a2, 32, 1))
+        return carry
+
+    lax.fori_loop(0, TERMS, build, 0)
+    left16[...] = left[...].astype(BF16)
+
     arrived(cr, 8, 8)
     collect(ops1)
     laplace(v1, halos1)
@@ -327,7 +337,7 @@
 
     operate(relax)
 
-    halos2 = (xlo2, xhi2, ylo2, yhi2, z2)
+    halos2 = (xlo2, xhi2, ylo2, yhi2, z2, zfull)
     ops2 = spread(v2, ysend2, halos2, 14)
     for j in range(4):
         for v in range(8):
@@ -336,6 +346,17 @@
     here = 2 * side + core
     for j in range(4):
         copy(piece(bs, j), piece(br, here), 19 + j, 19 + here, owner(j)).start()
+    row = lax.broadcasted_iota(jnp.int32, (256, 256), 0)
+    col = lax.broadcasted_iota(jnp.int32, (256, 256), 1)
+    half = jnp.bitwise_and(lax.shift_right_logical(row, 6), 1)
+    b_row = 2 * half + lax.shift_right_logical(row, 7)
+    z_row = jnp.bitwise_and(row, 63)
+    off = z_row - 2 * jnp.bitwise_and(col, 31)
+    near = jnp.where(off == 0, 0.5, jnp.where(jnp.logical_or(off == 1, off == -1), 0.25, 0.0))
+    main_w = jnp.where(jnp.logical_and(col < 128, lax.shift_right_logical(col, 5) == b_row), near, 0.0)
+    next_w = jnp.where(jnp.logical_and(col == 128 + b_row, z_row == 63), 0.25, 0.0)
+    wz[...] = (main_w + next_w).astype(BF16)
+
     collect(ops2)
     laplace(v2, halos2)
 
@@ -473,10 +494,12 @@
     def rows(n, width=128, kind=F32):
         return pltpu.VMEM((n, width), kind)
 
-    halos = [rows(4 * VEC), rows(4 * VEC), rows(VEC), rows(VEC), rows(VEC)]
+    halos = [rows(4 * VEC), rows(4 * VEC), rows(VEC), rows(VEC), rows(16)]
     return [
+        rows(SL * 32), rows(SL * 32), rows(32), rows(TERMS * 32), pltpu.VMEM((TERMS, 3, 4 * SL), jnp.int32),
+        pltpu.VMEM((TERMS, 3, 4 * SL), F32), pltpu.SemaphoreType.DMA((6,)),
         rows(4 * OWN), rows(4 * OWN), rows(8 * (TERMS + 1)), rows(4 * OWN), rows(4 * OWN), rows(8 * (TERMS + 1)),
-        rows(ALL), rows(ALL), *halos, *halos, rows(3 * VEC), rows(3 * VEC), rows(ALL), rows(4 * 256, 256, BF16),
+        rows(ALL), rows(ALL), *halos, *halos, rows(VEC), rows(2 * VEC + 16), rows(2 * VEC + 16), rows(ALL), rows(4 * 256, 256, BF16),
         rows(TERMS * VEC, 256), rows(TERMS * VEC, 256, BF16), rows(128), rows(128), rows(ALL), rows(ALL), rows(256, 256, BF16),
         rows(4 * OWN), rows(4 * OWN), rows(8 * VEC, 256), rows(2 * VEC), rows(2 * VEC), rows(2 * VEC), rows(VEC),
         rows(VEC), rows(2 * VEC), rows(160), rows(160),
@@ -489,7 +512,7 @@
     smoothed, coarse = pl.pallas_call(
         kernel,
         out_shape=(jax.ShapeDtypeStruct((SL * 32, 128), F32), jax.ShapeDtypeStruct((SL * 8, 128), F32)),
-        in_specs=[whole] * 6,
+        in_specs=[pl.BlockSpec(memory_space=pl.ANY)] * 6,
         out_specs=(whole, whole),
         scratch_shapes=scratch(),
         compiler_params=pltpu.CompilerParams(collective_id=0, has_side_effects=True),

time: 54.3 us -> 52.4 us (0.965)
  the two profiles are of different devices: /device:TPU:23 before, /device:TPU:15 now
where the time goes in v2:
time: 52.4 us; the launch traced here: 52.2 us
  Pallas kernels  49.2 us (94%)
  local copies, waits for them, and re-layouts  2.35 us (4%)
  between operations  0.65 us (1%)
    pallas_call x1, Pallas kernels, body(): pl.pallas_call(kernel, out_shape=(jax.ShapeDtypeStruct((SL * 32, 128), F3...  49.2 us
    unnamed x4, local copies, waits for them, and re-layouts  2.35 us

profile of v2, /device:TPU:15, one launch (start us, length us, event | category | flops | bytes accessed | tf_op | source)
XLA Modules:
  0.0 52.2 jit_solution(9812123641129217889)
XLA Ops:
  0.6 49.2 %sweep.1 = (f32[544,128]{1,0:T(8,128)}, f32[136,128]{1,0:T(8,128)}) custom-call(f32[544,128]{1,0:T(8,128)} %bitcast.9, f32[544,128]{1,0:T(8,128)} %bitcast.10, f32[32,128]{1,0:T(8,128)} %bitcast.16, f32[320,128]{1,0:T(8,128)} %bitcast.12, s32[10,3,68]{2,1,0:T(4,128)} %bitcast.14, f32[10,3,68]{2,1,0:T(4,128)} %bitcast.15), custom_call_target="tpu_custom_call" | custom-call | tf_op jit(solution)/shard_map/sweep/pallas_call | solution.py:512
  49.9 0.0 copy-start
  49.9 1.7 %copy.10 = f32[17,4,8,128]{3,2,1,0:T(8,128)} copy(f32[17,4,8,128]{3,2,1,0:T(8,128)} %bitcast.11) | data formatting | bytes 557056
  51.6 0.0 copy-done
  51.6 0.6 %copy.11 = f32[17,2,4,64]{3,2,1,0:T(4,128)} copy(f32[17,2,4,64]{3,2,1,0:T(4,128)S(1)} %bitcast.13) | data formatting | bytes 69632
Async XLA Ops:
  49.9 1.7 %copy-start = (f32[136,128]{1,0:T(8,128)S(1)}, f32[136,128]{1,0:T(8,128)}, u32[]{:S(2)}) copy-start(f32[136,128]{1,0:T(8,128)} %get-tuple-element.5) | copy-start | bytes 208900

commit v3 on v2

--- a/solution.py
+++ b/solution.py
@@ -30,7 +30,7 @@
     field_in, source_in, mean_in, var_in, cols_in, vals_in, smoothed, coarse,
     field, source, mean, var, cols, vals, loads,
     fs, ss, cs, fr, sr, cr, v1, v2, xlo1, xhi1, ylo1, yhi1, z1, xlo2, xhi2, ylo2, yhi2, z2, zfull,
-    ysend1, ysend2, lap, rhs, left, left16, gt, gt2, srcv, after, wz, bs, br, dbuf, cxs, cys, cxr, cyr, cxyr, fin, cbs, cbr,
+    ysend1, ysend2, lap, rhs, left, left16, gt, gt2, srcv, after, wz, bs, br, dbuf, cms, cxs, cys, cxys, cmr, cxr, cyr, cxyr,
     send, recv,
 ):
     gx, gy, ch = lax.axis_index("gx"), lax.axis_index("gy"), lax.axis_index("chaos")
@@ -60,8 +60,14 @@
     barrier = pltpu.get_barrier_semaphore()
     neighbours = [
         (has_xp, place(-1, 0)), (has_xn, place(1, 0)), (has_yp, place(0, -1)), (has_yn, place(0, 1)),
-        (jnp.logical_and(has_xp, has_yp), place(-1, -1)), (jnp.logical_and(has_xn, has_yn), place(1, 1)),
     ]
+    more_y, more_x = gy > 0, gx > 0
+    for s in range(2):
+        lower = ((gy + 1 + 4 * s) % 8) // 4 * 2
+        for c in range(2):
+            neighbours.append((more_y, (gx, (gy + 1) % 4, lower + c)))
+        neighbours.append((more_x, (gx - 1, far_gy, worker(s, 1)[2])))
+        neighbours.append((jnp.logical_and(more_x, more_y), (gx - 1, (gy + 1) % 4, lower + 1)))
     for j in range(4):
         pl.semaphore_signal(barrier, inc=1, device_id=owner(j), device_id_type=MESH)
     pl.semaphore_signal(barrier, inc=1, device_id=across, device_id_type=MESH)
@@ -108,7 +114,8 @@
 
     staged[0].wait()
     pack(field, fs)
-    pl.semaphore_wait(barrier, 5 + sum(jnp.where(cond, 1, 0) for cond, dev in neighbours))
+    pl.semaphore_wait(barrier, 5 + sum(jnp.where(cond, 1, 0) for cond, dev in neighbours[0:4])
+                      + jnp.where(has_yn, 4, 0) + 4 * core * jnp.where(has_xn, 1, 0) * jnp.where(has_yn, 2, 1))
 
     for c in range(2):
         for s in range(2):
@@ -144,17 +151,27 @@
             for ref in yref:
                 ref[...] = zero_vec
 
-    @pl.when(xi == 0)
+    def clear(ref, n, rows):
+        for r in rows:
+            ref[pl.ds(r * n, n), :] = jnp.zeros((n, 128), F32)
+
+    @pl.when(gx == 0)
     def _():
-        cxr[...] = jnp.zeros((2 * VEC, 128), F32)
-
-    @pl.when(blk == 0)
+        clear(cxr, 32, (0, 2))
+
+    @pl.when(gy == 0)
     def _():
-        cyr[...] = zero_vec
-
-    @pl.when(jnp.logical_or(xi == 0, blk == 0))
+        clear(cyr, 16, range(4))
+        clear(cxyr, 16, range(4))
+
+    @pl.when(jnp.logical_and(gx == 0, gy > 0))
     def _():
-        cxyr[...] = zero_vec
+        clear(cxyr, 16, (0, 2))
+
+    clear(cms, 32, range(4))
+    clear(cxs, 32, range(4))
+    clear(cys, 16, range(4))
+    clear(cxys, 16, range(4))
 
     lane72 = lanes(VEC)
     low = lane72 < 64
@@ -187,6 +204,14 @@
         yp = copy(down, yhi, base + 3, base + 3, place(0, -1))
         zc = copy(zs, z, base + 4, base + 4, across)
 
+        @pl.when(has_xn)
+        def _():
+            xn.start()
+
+        @pl.when(has_xp)
+        def _():
+            xp.start()
+
         total = zero_vec
         for v in range(8):
             total = jnp.where(z64 == v, pltpu.roll(vec(val, v), v + 65 * (1 - side), 1), total)
@@ -196,14 +221,6 @@
         stage[pl.ds(2 * VEC, 8), :] = packed
         stage[pl.ds(2 * VEC + 8, 8), :] = total[64:72]
         zc.start()
-
-        @pl.when(has_xn)
-        def _():
-            xn.start()
-
-        @pl.when(has_xp)
-        def _():
-            xp.start()
 
         up[...] = jnp.where(low, swing(vec(val, 3)), vec(val, 7))
         down[...] = jnp.where(low, vec(val, 0), swing(vec(val, 4)))
@@ -387,31 +404,48 @@
     def both(r):
         return parts[r * VEC:(r + 1) * VEC, 0:128], parts[r * VEC:(r + 1) * VEC, 128:256]
 
-    def one(r):
+    lane8 = lanes(8)
+
+    def wide(out, r):
         a, b = both(r)
-        return a + pltpu.roll(b, 32, 1)
-
-    a, b = both(1)
-    cxs[0:VEC, :] = a
-    cxs[VEC:2 * VEC, :] = b
-    cx = copy(cxs, cxr, 23, 23, place(1, 0))
-
-    @pl.when(has_xn)
-    def _():
-        cx.start()
-
-    cys[0:VEC, :] = one(2)
-    cys[VEC:2 * VEC, :] = one(3)
-    cy = copy(cys.at[pl.ds(0, VEC), :], cyr, 24, 24, place(0, 1))
-    cxy = copy(cys.at[pl.ds(VEC, VEC), :], cxyr, 25, 25, place(1, 1))
-
-    @pl.when(has_yn)
-    def _():
-        cy.start()
-
-    @pl.when(jnp.logical_and(has_xn, has_yn))
-    def _():
-        cxy.start()
+        for j in range(4):
+            out[pl.ds(j * 32, 16), :] = a[16 * j:16 * j + 16]
+            out[pl.ds(j * 32 + 16, 8), :] = jnp.where(
+                lane8 < 8, b[16 * j:16 * j + 8], pltpu.roll(b[16 * j + 8:16 * j + 16], 8, 1)
+            )
+            out[pl.ds(j * 32 + 24, 1), :] = a[64 + j:65 + j]
+            out[pl.ds(j * 32 + 25, 1), :] = b[64 + j:65 + j]
+
+    def slim(out, r):
+        a, b = both(r)
+        w = a + pltpu.roll(b, 32, 1)
+        for j in range(4):
+            out[pl.ds(j * 16, 8), :] = w[16 * j:16 * j + 8] + pltpu.roll(w[16 * j + 8:16 * j + 16], 64, 1)
+            out[pl.ds(j * 16 + 8, 1), :] = w[64 + j:65 + j]
+
+    def cut(ref, i, n):
+        return ref.at[pl.ds(pl.multiple_of(i * n, 8), n), :]
+
+    def parted(src, dst, n, base, slot, dx, dy):
+        return [
+            copy(cut(src, j, n), cut(dst, slot, n), base + j, base + slot, (gx + dx, far_gy + dy, j)) for j in range(4)
+        ]
+
+    there = 2 * side + 1 - core
+    has_xyn = jnp.logical_and(has_xn, has_yn)
+    results = []
+    for fill, r, src, dst, n, base, slot, dx, dy, cond in (
+        (wide, 1, cxs, cxr, 32, 30, there, core, 0, has_xn), (slim, 3, cxys, cxyr, 16, 38, there, core, 1, has_xyn),
+        (slim, 2, cys, cyr, 16, 34, here, 0, 1, has_yn), (wide, 0, cms, cmr, 32, 26, here, 0, 0, gx >= 0),
+    ):
+        fill(src, r)
+        ops = parted(src, dst, n, base, slot, dx, dy)
+        results.append((cond, ops))
+
+        @pl.when(cond)
+        def _():
+            for op in ops:
+                op.start()
 
     for j in range(4):
         arrived(piece(br, j), 19 + j, 19 + j)
@@ -428,55 +462,50 @@
         smoothed[pl.ds(512 + x * 8, 4), :] = jnp.where(low8, ta, swing(tb))[4 * xl:4 * xl + 4]
         smoothed[pl.ds(512 + x * 8 + 4, 4), :] = jnp.where(low8, swing(ta), tb)[4 * xl:4 * xl + 4]
 
-    a, b = both(0)
-
-    @pl.when(has_xp)
-    def _():
-        cx.wait_recv()
-
-    @pl.when(has_yp)
-    def _():
-        cy.wait_recv()
-
-    @pl.when(jnp.logical_and(has_xp, has_yp))
-    def _():
-        cxy.wait_recv()
-
-    ysum = cyr[...] + cxyr[...]
-    fin[0:VEC, :] = a + cxr[0:VEC, :] + jnp.where(lane72 < 32, ysum, 0.0)
-    fin[VEC:2 * VEC, :] = b + cxr[VEC:2 * VEC, :] + jnp.where(lane72 == 0, pltpu.roll(ysum, 96, 1), 0.0)
-    for j in range(4):
-        cbs[pl.ds(j * 40, 16), :] = fin[pl.ds(16 * j, 16), :]
-        cbs[pl.ds(j * 40 + 16, 16), :] = fin[pl.ds(VEC + 16 * j, 16), :]
-        cbs[pl.ds(j * 40 + 32, 2), :] = fin[pl.ds(64 + j, 2, stride=VEC), :]
-        cbs[pl.ds(j * 40 + 34, 6), :] = jnp.zeros((6, 128), F32)
-
-    def small(ref, i):
-        return ref.at[pl.ds(pl.multiple_of(i * 40, 8), 40), :]
-
-    for j in range(4):
-        copy(small(cbs, j), small(cbr, here), 26 + j, 26 + here, owner(j)).start()
-    for j in range(4):
-        arrived(small(cbr, j), 26 + j, 26 + j)
+    for i in range(4):
+        arrived(cut(cmr, i, 32), 26, 26 + i)
+
+        @pl.when(more_x if i % 2 == 0 else gx >= 0)
+        def _():
+            arrived(cut(cxr, i, 32), 30, 30 + i)
+
+        @pl.when(more_y)
+        def _():
+            arrived(cut(cyr, i, 16), 34, 34 + i)
+
+        @pl.when(jnp.logical_and(more_x, more_y) if i % 2 == 0 else more_y)
+        def _():
+            arrived(cut(cxyr, i, 16), 38, 38 + i)
+
     lane16 = lanes(16)
+
+    def unite(i):
+        m = cmr[pl.ds(i * 32, 16), :] + cxr[pl.ds(i * 32, 16), :]
+        zp = cmr[pl.ds(i * 32 + 16, 8), :] + cxr[pl.ds(i * 32 + 16, 8), :]
+        t = cmr[pl.ds(i * 32 + 24, 8), :] + cxr[pl.ds(i * 32 + 24, 8), :]
+        yp = cyr[pl.ds(i * 16, 8), :] + cxyr[pl.ds(i * 16, 8), :]
+        yt = cyr[pl.ds(i * 16 + 8, 8), :] + cxyr[pl.ds(i * 16 + 8, 8), :]
+        z = jnp.concatenate([zp, pltpu.roll(zp, 120, 1)], 0)
+        y = jnp.concatenate([yp, swing(yp)], 0)
+        m = m + jnp.where(lane16 < 32, y, 0.0)
+        return m, z, y, t + jnp.where(lane8 < 32, yt, 0.0), pltpu.roll(t, 7, 0), yt
+
     for x in range(2):
-        ma, mb = cbr[pl.ds(x * 40, 16), :], cbr[pl.ds((2 + x) * 40, 16), :]
-        za = cbr[pl.ds(x * 40 + 16, 16), :]
-        tl, tr = cbr[pl.ds(x * 40 + 32, 8), :], cbr[pl.ds((2 + x) * 40 + 32, 8), :]
+        ma, za, ya, ta, zt, yt = unite(x)
+        mb, _, _, tb, _, _ = unite(2 + x)
         for b in range(4):
-            def joined(left_, right_, extra, lane):
+            def joined(left_, right_, extra, edge_y, lane):
                 out = jnp.where(lane < 32, pltpu.roll(left_, (128 - 32 * b) % 128, 1), pltpu.roll(right_, (160 - 32 * b) % 128, 1))
-                return out + jnp.where(lane == 32, pltpu.roll(extra, 32 - b, 1), 0.0)
-
-            coarse[pl.ds(x * 4 + b, 16, stride=8), :] = joined(ma, mb, za, lane16)
-            t = joined(tl, tr, pltpu.roll(tl, 7, 0), lanes(8))
-            coarse[pl.ds(128 + x * 4 + b, 1), :] = t[0:1]
+                extra = pltpu.roll(extra, 32 - b, 1)
+                return out + jnp.where(lane == 32, extra + edge_y if b == 0 else extra, 0.0)
+
+            coarse[pl.ds(x * 4 + b, 16, stride=8), :] = joined(ma, mb, za, ya, lane16)
+            coarse[pl.ds(128 + x * 4 + b, 1), :] = joined(ta, tb, zt, yt, lane8)[0:1]
 
     for j in range(4):
         copy(piece(fs, j), piece(fr, j), j, j, across).wait_send()
         copy(piece(ss, j), piece(sr, j), 4 + j, 4 + j, across).wait_send()
         copy(piece(bs, j), piece(br, j), 19 + j, 19 + j, across).wait_send()
-        copy(small(cbs, j), small(cbr, j), 26 + j, 26 + j, across).wait_send()
     coefs.wait_send()
     for xn, xp, yn, yp, zc in (ops1, ops2):
         zc.wait_send()
@@ -484,10 +513,11 @@
             @pl.when(cond)
             def _():
                 op.wait_send()
-    for cond, op in ((has_xn, cx), (has_yn, cy), (jnp.logical_and(has_xn, has_yn), cxy)):
+    for cond, ops in results:
         @pl.when(cond)
         def _():
-            op.wait_send()
+            for op in ops:
+                op.wait_send()
 
 
 def scratch():
@@ -501,17 +531,27 @@
         rows(4 * OWN), rows(4 * OWN), rows(8 * (TERMS + 1)), rows(4 * OWN), rows(4 * OWN), rows(8 * (TERMS + 1)),
         rows(ALL), rows(ALL), *halos, *halos, rows(VEC), rows(2 * VEC + 16), rows(2 * VEC + 16), rows(ALL), rows(4 * 256, 256, BF16),
         rows(TERMS * VEC, 256), rows(TERMS * VEC, 256, BF16), rows(128), rows(128), rows(ALL), rows(ALL), rows(256, 256, BF16),
-        rows(4 * OWN), rows(4 * OWN), rows(8 * VEC, 256), rows(2 * VEC), rows(2 * VEC), rows(2 * VEC), rows(VEC),
-        rows(VEC), rows(2 * VEC), rows(160), rows(160),
-        pltpu.SemaphoreType.DMA((30,)), pltpu.SemaphoreType.DMA((30,)),
+        rows(4 * OWN), rows(4 * OWN), rows(8 * VEC, 256), rows(128), rows(128), rows(64), rows(64),
+        rows(128), rows(128), rows(64), rows(64),
+        pltpu.SemaphoreType.DMA((42,)), pltpu.SemaphoreType.DMA((42,)),
     ]
+
+
+def store(smoothed, coarse, smoothed_out, coarse_out, sems):
+    ops = [
+        pltpu.make_async_copy(smoothed, smoothed_out, sems.at[0]), pltpu.make_async_copy(coarse, coarse_out, sems.at[1]),
+    ]
+    for op in ops:
+        op.start()
+    for op in ops:
+        op.wait()
 
 
 def body(field, source, mean_coef, var_coefs, galerkin_cols, galerkin_vals):
     whole = pl.BlockSpec(memory_space=pltpu.VMEM)
     smoothed, coarse = pl.pallas_call(
         kernel,
-        out_shape=(jax.ShapeDtypeStruct((SL * 32, 128), F32), jax.ShapeDtypeStruct((SL * 8, 128), F32)),
+        out_shape=(pltpu.VMEM((SL * 32, 128), F32), pltpu.VMEM((SL * 8, 128), F32)),
         in_specs=[pl.BlockSpec(memory_space=pl.ANY)] * 6,
         out_specs=(whole, whole),
         scratch_shapes=scratch(),
@@ -521,6 +561,15 @@
         field.reshape(SL * 32, 128), source.reshape(SL * 32, 128), mean_coef.reshape(32, 128),
         var_coefs.reshape(TERMS * 32, 128), jnp.swapaxes(galerkin_cols, 1, 2), jnp.swapaxes(galerkin_vals, 1, 2),
     )
+    anywhere = pl.BlockSpec(memory_space=pl.ANY)
+    smoothed, coarse = pl.pallas_call(
+        store,
+        out_shape=(jax.ShapeDtypeStruct((SL * 32, 128), F32), jax.ShapeDtypeStruct((SL * 8, 128), F32)),
+        in_specs=[whole] * 2,
+        out_specs=(anywhere, anywhere),
+        scratch_shapes=[pltpu.SemaphoreType.DMA((2,))],
+        name="store",
+    )(pltpu.with_memory_space_constraint(smoothed, pltpu.VMEM), pltpu.with_memory_space_constraint(coarse, pltpu.VMEM))
     return smoothed.reshape(field.shape), coarse[:, 0:64].reshape(SL, 2, 4, 64)
 
 

time: 52.4 us -> 46.8 us (0.89)
  Pallas kernels: 49.2 us -> 46 us
  local copies, waits for them, and re-layouts: 2.35 us -> 0 us
    pallas_call x1 -> x2, Pallas kernels: 49.2 us -> 46 us  [the longest x1 45.2 us: body(): pl.pallas_call(kernel, out_shape=(pltpu.VMEM((SL * 32, 128), F32), pltpu....]
    unnamed x4 -> x0, local copies, waits for them, and re-layouts: 2.35 us -> none
where the time goes in v3:
time: 46.8 us; the launch traced here: 46.6 us
  Pallas kernels  46 us (98%)
  between operations  0.64 us (1%)
    pallas_call x1, Pallas kernels, body(): pl.pallas_call(kernel, out_shape=(pltpu.VMEM((SL * 32, 128), F32), pltpu....  45.2 us

profile of v3, /device:TPU:15, one launch (start us, length us, event | category | flops | bytes accessed | tf_op | source)
XLA Modules:
  0.0 46.6 jit_solution(3149947670587562946)
XLA Ops:
  0.6 45.2 %sweep.1 = (f32[544,128]{1,0:T(8,128)S(1)}, f32[136,128]{1,0:T(8,128)S(1)}) custom-call(f32[544,128]{1,0:T(8,128)} %bitcast.9, f32[544,128]{1,0:T(8,128)} %bitcast.10, f32[32,128]{1,0:T(8,128)} %bitcast.14, f32[320,128]{1,0:T(8,128)} %bitcast.11, s32[10,3,68]{2,1,0:T(4,128)} %bitcast.12, f32[10,3,68]{2,1,0:T(4,128)} %bitcast.13), custom_call_target="tpu_custom_call" | custom-call | tf_op jit(solution)/shard_map/sweep/pallas_call | solution.py:552
  45.9 0.7 %store.1 = (f32[544,128]{1,0:T(8,128)}, f32[136,128]{1,0:T(8,128)}) custom-call(f32[544,128]{1,0:T(8,128)S(1)} %get-tuple-element.6.smoothed, f32[136,128]{1,0:T(8,128)S(1)} %get-tuple-element.7.coarse), custom_call_target="tpu_custom_call" | custom-call | tf_op jit(solution)/shard_map/store/pallas_call | solution.py:565

commit v4 on v3

--- a/solution.py
+++ b/solution.py
@@ -76,12 +76,16 @@
         def _():
             pl.semaphore_signal(barrier, inc=1, device_id=dev, device_id_type=MESH)
 
+    def plane_pair(ref, c):
+        return ref.reshape(SL, 32, 128).at[:, pl.ds(16 * c, 16), :]
+
     pairs = (
-        (field_in, field), (var_in, var), (mean_in, mean), (source_in, source), (cols_in, cols), (vals_in, vals),
+        (plane_pair(field_in, 0), plane_pair(field, 0)), (var_in, var), (mean_in, mean), (source_in, source), (cols_in, cols), (vals_in, vals),
+        (plane_pair(field_in, 1), plane_pair(field, 1)),
     )
     staged = [pltpu.make_async_copy(a, b, loads.at[i]) for i, (a, b) in enumerate(pairs)]
-    for op in staged:
-        op.start()
+    for i in (0, 6, 1, 2, 3, 4, 5):
+        staged[i].start()
 
     keep = (lax.broadcasted_iota(jnp.int32, (16, 128), 0) + SL * ch < P_SIZE)
     keep_tail = SL * ch + 16 < P_SIZE
@@ -91,8 +95,8 @@
         r = pltpu.roll(swing(t), 4, 0)
         return jnp.where(low8, t, r), swing(jnp.where(low8, r, t))
 
-    def pack(ref, out):
-        for x in range(4):
+    def pack(ref, out, planes=range(4)):
+        for x in planes:
             c, xl = x // 2, x % 2
             for y in range(4):
                 v = xl * 4 + y
@@ -113,11 +117,14 @@
         )
 
     staged[0].wait()
-    pack(field, fs)
+    pack(field, fs, (0, 1))
     pl.semaphore_wait(barrier, 5 + sum(jnp.where(cond, 1, 0) for cond, dev in neighbours[0:4])
                       + jnp.where(has_yn, 4, 0) + 4 * core * jnp.where(has_xn, 1, 0) * jnp.where(has_yn, 2, 1))
 
     for c in range(2):
+        if c == 1:
+            staged[6].wait()
+            pack(field, fs, (2, 3))
         for s in range(2):
             copy(piece(fs, 2 * s + c), piece(fr, ch), 2 * s + c, ch, worker(s, c)).start()
 
@@ -136,9 +143,6 @@
 
     staged[3].wait()
     pack(source, ss)
-    for c in range(2):
-        for s in range(2):
-            copy(piece(ss, 2 * s + c), piece(sr, ch), 4 + 2 * s + c, 4 + ch, worker(s, c)).start()
 
     zero_vec = jnp.zeros((VEC, 128), F32)
     for cond, xref, yref in ((xi == 0, (xlo1, xlo2), ()), (xi == last_x, (xhi1, xhi2), ()),
@@ -235,17 +239,20 @@
 
         return xn, xp, yn, yp, zc
 
+    def collect_x(ops):
+        xn, xp, yn, yp, zc = ops
+
+        @pl.when(has_xp)
+        def _():
+            xn.wait_recv()
+
+        @pl.when(has_xn)
+        def _():
+            xp.wait_recv()
+
     def collect(ops):
         xn, xp, yn, yp, zc = ops
 
-        @pl.when(has_xp)
-        def _():
-            xn.wait_recv()
-
-        @pl.when(has_xn)
-        def _():
-            xp.wait_recv()
-
         @pl.when(has_yp)
         def _():
             yn.wait_recv()
@@ -256,7 +263,7 @@
 
         zc.wait_recv()
 
-    def laplace(val, halos):
+    def laplace(val, halos, ops):
         xlo, xhi, ylo, yhi, zpacked, z = halos
         for t in range(8):
             z[pl.ds(8 * t, 8), :] = pltpu.roll(zpacked[0:8, :], (128 - 8 * t) % 128, 1) if t else zpacked[0:8, :]
@@ -265,7 +272,7 @@
             for y in range(4):
                 v = 4 * x + y
                 here = vec(val, v)
-                beside = (vec(val, v - 4) if x else vec(xlo, y)) + (vec(xhi, y) if x else vec(val, v + 4))
+                beside = vec(val, v - 4) if x else vec(val, v + 4)
                 if y > 0:
                     beside = beside + vec(val, v - 1)
                 elif x == 0:
@@ -283,6 +290,12 @@
                 beside = beside + jnp.where(edge_lane, pltpu.roll(z[...], (edge + 128 - v) % 128, 1), 0.0)
                 out = 6.0 * here - beside
                 lap[pl.ds(v * VEC, VEC), :] = out
+        collect_x(ops)
+        for x in range(2):
+            for y in range(4):
+                v = 4 * x + y
+                out = vec(lap, v) - vec(xhi if x else xlo, y)
+                lap[pl.ds(v * VEC, VEC), :] = out
                 b1 = out.astype(BF16)
                 b2 = (out - b1.astype(F32)).astype(BF16)
                 r, h = (v // 2) * 256, (v % 2) * 128
@@ -305,13 +318,16 @@
                 use(rows, m, total)
             return carry
 
-        lax.fori_loop(0, 4, step, 0)
+        lax.fori_loop(0, 4, step, 0, unroll=4)
 
     for j in range(4):
         arrived(piece(fr, j), j, j)
     gather(fr, v1)
     halos1 = (xlo1, xhi1, ylo1, yhi1, z1, zfull)
     ops1 = spread(v1, ysend1, halos1, 9)
+    for c in range(2):
+        for s in range(2):
+            copy(piece(ss, 2 * s + c), piece(sr, ch), 4 + 2 * s + c, 4 + ch, worker(s, c)).start()
     rhs[...] = jnp.zeros((4 * 256, 256), BF16)
     gt[...] = jnp.zeros((128, 128), F32)
     staged[4].wait()
@@ -343,16 +359,18 @@
 
     arrived(cr, 8, 8)
     collect(ops1)
-    laplace(v1, halos1)
+    laplace(v1, halos1, ops1)
+
+    def keep_total(rows, m, total):
+        after[rows, :] = total
+
+    operate(keep_total)
     for j in range(4):
         arrived(piece(sr, j), 4 + j, 4 + j)
     gather(sr, srcv)
-
-    def relax(rows, m, total):
-        first = srcv[rows, :] - total
-        v2[rows, :] = v1[rows, :] + (2.0 / 3.0) * first / (6.0 * m)
-
-    operate(relax)
+    for v in range(8):
+        first = vec(srcv, v) - vec(after, v)
+        v2[pl.ds(v * VEC, VEC), :] = vec(v1, v) + (2.0 / 3.0) * first / (6.0 * cr[pl.ds(TERMS * 8 + v, 1), :])
 
     halos2 = (xlo2, xhi2, ylo2, yhi2, z2, zfull)
     ops2 = spread(v2, ysend2, halos2, 14)
@@ -375,7 +393,7 @@
     wz[...] = (main_w + next_w).astype(BF16)
 
     collect(ops2)
-    laplace(v2, halos2)
+    laplace(v2, halos2, ops2)
 
     def residual(rows, m, total):
         after[rows, :] = srcv[rows, :] - total
@@ -527,7 +545,7 @@
     halos = [rows(4 * VEC), rows(4 * VEC), rows(VEC), rows(VEC), rows(16)]
     return [
         rows(SL * 32), rows(SL * 32), rows(32), rows(TERMS * 32), pltpu.VMEM((TERMS, 3, 4 * SL), jnp.int32),
-        pltpu.VMEM((TERMS, 3, 4 * SL), F32), pltpu.SemaphoreType.DMA((6,)),
+        pltpu.VMEM((TERMS, 3, 4 * SL), F32), pltpu.SemaphoreType.DMA((7,)),
         rows(4 * OWN), rows(4 * OWN), rows(8 * (TERMS + 1)), rows(4 * OWN), rows(4 * OWN), rows(8 * (TERMS + 1)),
         rows(ALL), rows(ALL), *halos, *halos, rows(VEC), rows(2 * VEC + 16), rows(2 * VEC + 16), rows(ALL), rows(4 * 256, 256, BF16),
         rows(TERMS * VEC, 256), rows(TERMS * VEC, 256, BF16), rows(128), rows(128), rows(ALL), rows(ALL), rows(256, 256, BF16),

time: 46.8 us -> 45.5 us (0.972)
  Pallas kernels: 46 us -> 44.7 us
    pallas_call x1, Pallas kernels: 45.2 us -> 44 us  [body(): pl.pallas_call(kernel, out_shape=(pltpu.VMEM((SL * 32, 128), F32), pltpu....]
where the time goes in v4:
time: 45.5 us; the launch traced here: 45.4 us
  Pallas kernels  44.7 us (98%)
  between operations  0.64 us (1%)
    pallas_call x1, Pallas kernels, body(): pl.pallas_call(kernel, out_shape=(pltpu.VMEM((SL * 32, 128), F32), pltpu....  44 us

profile of v4, /device:TPU:15, one launch (start us, length us, event | category | flops | bytes accessed | tf_op | source)
XLA Modules:
  0.0 45.4 jit_solution(11732266156025965308)
XLA Ops:
  0.6 44.0 %sweep.1 = (f32[544,128]{1,0:T(8,128)S(1)}, f32[136,128]{1,0:T(8,128)S(1)}) custom-call(f32[544,128]{1,0:T(8,128)} %bitcast.9, f32[544,128]{1,0:T(8,128)} %bitcast.10, f32[32,128]{1,0:T(8,128)} %bitcast.14, f32[320,128]{1,0:T(8,128)} %bitcast.11, s32[10,3,68]{2,1,0:T(4,128)} %bitcast.12, f32[10,3,68]{2,1,0:T(4,128)} %bitcast.13), custom_call_target="tpu_custom_call" | custom-call | tf_op jit(solution)/shard_map/sweep/pallas_call | solution.py:570
  44.6 0.7 %store.1 = (f32[544,128]{1,0:T(8,128)}, f32[136,128]{1,0:T(8,128)}) custom-call(f32[544,128]{1,0:T(8,128)S(1)} %get-tuple-element.6.smoothed, f32[136,128]{1,0:T(8,128)S(1)} %get-tuple-element.7.coarse), custom_call_target="tpu_custom_call" | custom-call | tf_op jit(solution)/shard_map/store/pallas_call | solution.py:583

commit v5 on v4

--- a/solution.py
+++ b/solution.py
@@ -30,7 +30,7 @@
     field_in, source_in, mean_in, var_in, cols_in, vals_in, smoothed, coarse,
     field, source, mean, var, cols, vals, loads,
     fs, ss, cs, fr, sr, cr, v1, v2, xlo1, xhi1, ylo1, yhi1, z1, xlo2, xhi2, ylo2, yhi2, z2, zfull,
-    ysend1, ysend2, lap, rhs, left, left16, gt, gt2, srcv, after, wz, bs, br, dbuf, cms, cxs, cys, cxys, cmr, cxr, cyr, cxyr,
+    ysend1, ysend2, lap, rhs, left, left16, gt, gt2, srcv, after, wz, bs, br, dbuf, factor, cms, cxs, cys, cxys, cmr, cxr, cyr, cxyr,
     send, recv,
 ):
     gx, gy, ch = lax.axis_index("gx"), lax.axis_index("gy"), lax.axis_index("chaos")
@@ -318,7 +318,7 @@
                 use(rows, m, total)
             return carry
 
-        lax.fori_loop(0, 4, step, 0, unroll=4)
+        lax.fori_loop(0, 4, step, 0, unroll=2)
 
     for j in range(4):
         arrived(piece(fr, j), j, j)
@@ -365,21 +365,24 @@
         after[rows, :] = total
 
     operate(keep_total)
+    factor[...] = (2.0 / 3.0) / (6.0 * cr[pl.ds(TERMS * 8, 8), :])
     for j in range(4):
         arrived(piece(sr, j), 4 + j, 4 + j)
-    gather(sr, srcv)
+        for v in range(8):
+            rows = pl.ds(v * VEC + 16 * j, 16)
+            v2[rows, :] = v1[rows, :] + factor[pl.ds(v, 1), :] * (sr[pl.ds(j * OWN + 16 * v, 16), :] - after[rows, :])
     for v in range(8):
-        first = vec(srcv, v) - vec(after, v)
-        v2[pl.ds(v * VEC, VEC), :] = vec(v1, v) + (2.0 / 3.0) * first / (6.0 * cr[pl.ds(TERMS * 8 + v, 1), :])
+        rows = pl.ds(v * VEC + 64, 4)
+        v2[rows, :] = v1[rows, :] + factor[pl.ds(v, 1), :] * (sr[pl.ds(128 + v, 4, stride=OWN), :] - after[rows, :])
+        v2[pl.ds(v * VEC + 68, 4), :] = jnp.zeros((4, 128), F32)
 
     halos2 = (xlo2, xhi2, ylo2, yhi2, z2, zfull)
     ops2 = spread(v2, ysend2, halos2, 14)
+    here = 2 * side + core
     for j in range(4):
         for v in range(8):
             bs[pl.ds(j * OWN + 16 * v, 16), :] = v2[pl.ds(v * VEC + 16 * j, 16), :]
         bs[pl.ds(j * OWN + 128, 8), :] = v2[pl.ds(64 + j, 8, stride=VEC), :]
-    here = 2 * side + core
-    for j in range(4):
         copy(piece(bs, j), piece(br, here), 19 + j, 19 + here, owner(j)).start()
     row = lax.broadcasted_iota(jnp.int32, (256, 256), 0)
     col = lax.broadcasted_iota(jnp.int32, (256, 256), 1)
@@ -392,6 +395,7 @@
     next_w = jnp.where(jnp.logical_and(col == 128 + b_row, z_row == 63), 0.25, 0.0)
     wz[...] = (main_w + next_w).astype(BF16)
 
+    gather(sr, srcv)
     collect(ops2)
     laplace(v2, halos2, ops2)
 
@@ -549,7 +553,7 @@
         rows(4 * OWN), rows(4 * OWN), rows(8 * (TERMS + 1)), rows(4 * OWN), rows(4 * OWN), rows(8 * (TERMS + 1)),
         rows(ALL), rows(ALL), *halos, *halos, rows(VEC), rows(2 * VEC + 16), rows(2 * VEC + 16), rows(ALL), rows(4 * 256, 256, BF16),
         rows(TERMS * VEC, 256), rows(TERMS * VEC, 256, BF16), rows(128), rows(128), rows(ALL), rows(ALL), rows(256, 256, BF16),
-        rows(4 * OWN), rows(4 * OWN), rows(8 * VEC, 256), rows(128), rows(128), rows(64), rows(64),
+        rows(4 * OWN), rows(4 * OWN), rows(8 * VEC, 256), rows(8), rows(128), rows(128), rows(64), rows(64),
         rows(128), rows(128), rows(64), rows(64),
         pltpu.SemaphoreType.DMA((42,)), pltpu.SemaphoreType.DMA((42,)),
     ]

time: 45.5 us -> 45.7 us (level)
  no operation moved by 1% of the time
where the time goes in v5:
time: 45.7 us; the launch traced here: 45.5 us
  Pallas kernels  44.9 us (98%)
  between operations  0.64 us (1%)
    pallas_call x1, Pallas kernels, body(): pl.pallas_call(kernel, out_shape=(pltpu.VMEM((SL * 32, 128), F32), pltpu....  44.1 us

profile of v5, /device:TPU:15, one launch (start us, length us, event | category | flops | bytes accessed | tf_op | source)
XLA Modules:
  0.0 45.5 jit_solution(4215143519978181359)
XLA Ops:
  0.6 44.1 %sweep.1 = (f32[544,128]{1,0:T(8,128)S(1)}, f32[136,128]{1,0:T(8,128)S(1)}) custom-call(f32[544,128]{1,0:T(8,128)} %bitcast.9, f32[544,128]{1,0:T(8,128)} %bitcast.10, f32[32,128]{1,0:T(8,128)} %bitcast.14, f32[320,128]{1,0:T(8,128)} %bitcast.11, s32[10,3,68]{2,1,0:T(4,128)} %bitcast.12, f32[10,3,68]{2,1,0:T(4,128)} %bitcast.13), custom_call_target="tpu_custom_call" | custom-call | tf_op jit(solution)/shard_map/sweep/pallas_call | solution.py:574
  44.8 0.7 %store.1 = (f32[544,128]{1,0:T(8,128)}, f32[136,128]{1,0:T(8,128)}) custom-call(f32[544,128]{1,0:T(8,128)S(1)} %get-tuple-element.6.smoothed, f32[136,128]{1,0:T(8,128)S(1)} %get-tuple-element.7.coarse), custom_call_target="tpu_custom_call" | custom-call | tf_op jit(solution)/shard_map/store/pallas_call | solution.py:587
